TPU v7x, 32 devices: a whole 2x2x4 slice. The times are simulated.
32 devices in a mesh: dp: 4 (over z), ctx: 8 (over y, x, core).
Axes of the slice: x: 2, y: 2, z: 4, core: 2. Of those that a mesh axis runs over, the one named last changes fastest.
Arguments:
- queries: bfloat16 [4, 1024, 2048], P('dp', 'ctx'), may hold values from -6 to 6
- keys: bfloat16 [4, 1024, 2048], P('dp', 'ctx'), may hold values from -6 to 6
- values: bfloat16 [4, 1024, 2048], P('dp', 'ctx'), may hold values from -6 to 6
- out_grad: bfloat16 [4, 1024, 2048], P('dp', 'ctx'), may hold values from -96 to 96
- feature_weight: bfloat16 [16, 128, 128], replicated, may hold values from -0.5 to 0.5
- doc_lengths: int32 [4, 8], P('dp'), may hold values from 1 to 256, 1024 in all within a row
Outputs:
- grad_queries: bfloat16 [4, 1024, 2048], P('dp', 'ctx')
- grad_keys: bfloat16 [4, 1024, 2048], P('dp', 'ctx')
- grad_values: bfloat16 [4, 1024, 2048], P('dp', 'ctx')
- grad_weight: float32 [2048, 128], P(('dp', 'ctx'))
Inputs may be any that keep to these rules, and one draw needn't show every extreme that they name: `doc_lengths`: each pack's lengths sum to 1024, and the longest document of each pack has exactly 256 tokens.
All inputs are finite; a program needn't handle non-finite values.
Results may differ from a plain program's by a relative error of at most 0.0015.
Values sent between devices are 32-bit elements; how exact they have to be, the bound alone decides.
No kernel may reach another device: no remote copies, remote signals or barrier semaphores. Data moves between devices by JAX's collectives and lax.ppermute only.
A program may use at most 128 MiB of HBM per device.

v0:
```python
import math

import jax
import jax.numpy as jnp
from jax import lax
from jax.sharding import PartitionSpec as P


def carried_in(value, axis, combine, identity, reverse):
    peers, place = (lax.axis_size(axis), lax.axis_index(axis))
    everything = jax.tree.map(lambda part: lax.all_gather(part, axis), value)
    start = jax.tree.map(
        lambda part, zero: jnp.broadcast_to(jnp.asarray(zero, part.dtype), part.shape),
        value,
        identity,
    )

    def step(k, before):
        at = peers - 1 - k if reverse else k
        reached = at > place if reverse else at < place
        new = combine(before, jax.tree.map(lambda part: part[at], everything))
        return jax.tree.map(lambda a, b: jnp.where(reached, a, b), new, before)

    return lax.fori_loop(0, peers, step, start)


def einsum_high(form, *operands):
    return jnp.einsum(form, *operands, precision=lax.Precision.HIGHEST)


def block_scores(feat_q, feat_k, doc_ids):
    count = doc_ids.shape[0]
    causal = jnp.arange(count)[:, None] >= jnp.arange(count)[None, :]
    same_doc = doc_ids[:, None] == doc_ids[None, :]
    keep_mask = (causal & same_doc).astype(jnp.float32)
    scores = einsum_high("thi,shi->hts", feat_q, feat_k) * keep_mask[None]
    return (scores, keep_mask)


def join_states(earlier, later):
    cut = later[2]
    merged_state = jnp.where(cut > 0, later[0], earlier[0] + later[0])
    merged_norm = jnp.where(cut > 0, later[1], earlier[1] + later[1])
    return (merged_state, merged_norm, jnp.maximum(earlier[2], later[2]))


def shards(queries, keys, values, out_grad, feature_weight, doc_lengths):
    ctx_size = lax.axis_size("ctx")
    dp_size = lax.axis_size("dp")
    tok_rows = queries.shape[1]
    heads = feature_weight.shape[0]
    width = feature_weight.shape[1]
    offset = lax.axis_index("ctx") * tok_rows
    lengths = doc_lengths[0]
    starts = jnp.cumsum(lengths) - lengths

    def doc_of(points):
        return jnp.sum((starts[None, :] <= points[:, None]).astype(jnp.int32), axis=1) - 1

    positions = offset + jnp.arange(tok_rows, dtype=jnp.int32)
    doc_ids = doc_of(positions)
    borders = doc_of(jnp.stack([offset - 1, offset + tok_rows]))
    doc_before = borders[0]
    doc_after = borders[1]
    query_heads = queries[0].reshape(tok_rows, heads, width)
    key_heads = keys[0].reshape(tok_rows, heads, width)
    value_heads = values[0].reshape(tok_rows, heads, width).astype(jnp.float32)
    cotangent = out_grad[0].reshape(tok_rows, heads, width).astype(jnp.float32)
    pre_q = jnp.einsum(
        "thi,hij->thj", query_heads, feature_weight, preferred_element_type=jnp.float32
    )
    pre_k = jnp.einsum(
        "thi,hij->thj", key_heads, feature_weight, preferred_element_type=jnp.float32
    )
    feat_q = jax.nn.softplus(pre_q)
    feat_k = jax.nn.softplus(pre_k)
    weight32 = feature_weight.astype(jnp.float32)
    factor = 1.0 / math.sqrt(dp_size * ctx_size * tok_rows)
    scores, keep_mask = block_scores(feat_q, feat_k, doc_ids)
    tail = (doc_ids == doc_ids[-1]).astype(jnp.float32)[:, None, None]
    local_state = einsum_high("thi,the->hie", feat_k * tail, value_heads)
    local_norm = jnp.sum(feat_k * tail, axis=0)
    cut_before = (doc_ids[-1] != doc_before).astype(jnp.float32)
    empty_state = jnp.zeros((heads, width, width), jnp.float32)
    empty_norm = jnp.zeros((heads, width), jnp.float32)
    state_in, norm_in, unused = carried_in(
        (local_state, local_norm, cut_before),
        "ctx",
        join_states,
        (empty_state, empty_norm, jnp.float32(0.0)),
        False,
    )
    inside = (doc_ids == doc_before).astype(jnp.float32)[:, None]
    numer = einsum_high("hts,she->the", scores, value_heads) + inside[:, :, None] * einsum_high(
        "thi,hie->the", feat_q, state_in
    )
    denom = jnp.sum(scores, axis=2).T + inside * einsum_high("thi,hi->th", feat_q, norm_in)
    attn_out = numer / denom[:, :, None]
    scaled = cotangent / denom[:, :, None]
    shift_term = -jnp.sum(cotangent * attn_out, axis=2) / denom
    score_grad = (
        einsum_high("the,she->hts", scaled, value_heads) + shift_term.T[:, :, None]
    ) * keep_mask[None]
    grad_fq = einsum_high("hts,shi->thi", score_grad, feat_k) + inside[:, :, None] * (
        einsum_high("hie,the->thi", state_in, scaled) + shift_term[:, :, None] * norm_in[None]
    )
    grad_pre_q = grad_fq * jax.nn.sigmoid(pre_q)
    grad_query = einsum_high("thj,hij->thi", grad_pre_q, weight32)
    query_term = (
        einsum_high("thi,thj->hij", query_heads.astype(jnp.float32), grad_pre_q).reshape(
            heads * width, width
        )
        * factor
    )
    head_part = (doc_ids == doc_ids[0]).astype(jnp.float32)[:, None, None]
    local_rstate = einsum_high("thi,the->hie", feat_q * head_part, scaled)
    local_rnorm = einsum_high("thi,th->hi", feat_q * head_part, shift_term)
    cut_after = (doc_ids[0] != doc_after).astype(jnp.float32)
    rstate_in, rnorm_in, unused_too = carried_in(
        (local_rstate, local_rnorm, cut_after),
        "ctx",
        join_states,
        (empty_state, empty_norm, jnp.float32(0.0)),
        True,
    )
    later_in = (doc_ids == doc_after).astype(jnp.float32)[:, None, None]
    grad_fk = einsum_high("hts,thi->shi", score_grad, feat_q) + later_in * (
        einsum_high("hie,she->shi", rstate_in, value_heads) + rnorm_in[None]
    )
    grad_value = einsum_high("hts,the->she", scores, scaled) + later_in * einsum_high(
        "hie,shi->she", rstate_in, feat_k
    )
    grad_pre_k = grad_fk * jax.nn.sigmoid(pre_k)
    grad_key = einsum_high("thj,hij->thi", grad_pre_k, weight32)
    key_term = (
        einsum_high("thi,thj->hij", key_heads.astype(jnp.float32), grad_pre_k).reshape(
            heads * width, width
        )
        * factor
    )
    grad_weight = lax.psum_scatter(
        query_term + key_term, ("dp", "ctx"), scatter_dimension=0, tiled=True
    )
    flat_shape = (1, tok_rows, heads * width)
    return (
        grad_query.reshape(flat_shape).astype(jnp.bfloat16),
        grad_key.reshape(flat_shape).astype(jnp.bfloat16),
        grad_value.reshape(flat_shape).astype(jnp.bfloat16),
        grad_weight,
    )


def solution(mesh):
    placed = (
        P("dp", "ctx", None),
        P("dp", "ctx", None),
        P("dp", "ctx", None),
        P("dp", "ctx", None),
        P(),
        P("dp", None),
    )
    return jax.shard_map(
        shards,
        mesh=mesh,
        in_specs=placed,
        out_specs=(
            P("dp", "ctx", None),
            P("dp", "ctx", None),
            P("dp", "ctx", None),
            P(("dp", "ctx"), None),
        ),
        check_vma=False,
    )
```

profile of v0, /device:TPU:0, one launch (start us, length us, event | category | flops | bytes accessed | tf_op | source)
XLA Modules:
  0.0 335.6 jit_solution(15238799259815218909)
XLA Ops:
  13.1 2.5 compare_convert_fusion.1
  17.5 2.5 fusion.26
  24.6 15.7 %all-reduce.2 = (f32[8]{0:T(128)S(1)}, f32[8]{0:T(128)S(1)}) all-reduce(f32[8]{0:T(128)S(1)} %dynamic-update-slice, f32[8]{0:T(128)S(1)} %dynamic-update-slice.1), channel_id=1, replica_groups=mesh['dp'=4,'ctx'=8] {'ctx'}, use_global_device_ids=true, to_apply=%add | all-reduce | flops 16 | bytes 128
  42.8 8.4 %all-gather.1 = f32[128,128]{1,0:T(8,128)S(1)} all-gather(f32[16,128]{1,0:T(8,128)S(1)} %get-tuple-element.408), channel_id=3, replica_groups=mesh['dp'=4,'ctx'=8] {'ctx'}, dimensions={0}, use_global_device_ids=true | all-gather | bytes 73728 | tf_op jit(solution)/shard_map/all_gather | solution.py:11
  51.7 5.8 %fusion.43 = (f32[16,128]{1,0:T(8,128)S(1)}, f32[16,128,128]{1,2,0:T(8,128)}) fusion(f32[128,128]{0,1:T(8,128)S(1)} %fusion.36, f32[128,16,128]{2,0,1:T(8,128)} %copy-done.11, f32[128,16,128]{2,0,1:T(8,128)S(1)} %convolution_bitcast_fusion), kind=kOutput, calls=%fused_computation.80 | convolution fusion | flops 406321152 | bytes 3219456 | tf_op jit(solution)/shard_map/thi,shi->hts/dot_general | solution.py:28
  57.5 19.8 %all-gather.7.cloned.1.call-done = f32[128,128,128]{2,1,0:T(8,128)} async-done(((f32[16,128,128]{2,1,0:T(8,128)}), f32[128,128,128]{2,1,0:T(8,128)}) %all-gather.7.cloned.1.call-update) | async-done | bytes 8388624 | tf_op jit(solution)/shard_map/all_gather | solution.py:11
  77.3 25.2 %while.34 = (s32[]{:T(128)}, f32[16,128,128]{2,1,0:T(8,128)S(1)}, f32[16,128]{1,0:T(8,128)S(1)}, s32[]{:T(128)}, f32[8]{0:T(128)S(1)}, /*index=5*/f32[8,16,128,1...) while((s32[]{:T(128)}, f32[16,128,128]{2,1,0:T(8,128)S(1)}, ...), condition=%wide.region_6.7_spmd.clone, body=%wide.region_5.6_spmd.clone.sunk | while | flops 1056773 | bytes 3170458 | solution.py:24
  102.5 2.1 fusion.40
  104.6 4.6 %fusion.24 = f32[16,128,128]{2,1,0:T(8,128)} fusion(f32[128]{0:T(128)S(1)} %get-tuple-element.401, f32[128,16,128]{0,2,1:T(8,128)} %bitcast.143, f32[128,16]{0,1:T(8,128)S(1)} %fusion.37, f32[128,16,128]{2,0,1:T(8,128)S(1)} %convolution_bitcast_fusion), kind=kOutput, calls=%fused_computation.44 | convolution fusion | flops 404750336 | bytes 3154432 | tf_op jit(solution)/shard_map/thi,the->hie/dot_general | solution.py:28
  109.5 2.3 convolution_bitcast_fusion.5
  111.8 4.1 %fusion.21 = f32[128,16]{0,1:T(8,128)S(1)} fusion(f32[128,16,128]{0,2,1:T(8,128)} %bitcast.144, f32[128,16,128]{0,2,1:T(8,128)S(1)} %convolution_bitcast_fusion.5, f32[16,128,128]{2,1,0:T(8,128)S(1)} %get-tuple-element.307, f32[128]{0:T(128)S(1)} %get-tuple-element.402, f32[128,16]{0,1:T(8,128)S(1)} %fusion.37, f32[128,16,128]{2,0,1:T(8,128)} %copy-done.1), kind=kOutput, calls=%fused_computation.41 | convolution fusion | flops 405534720 | bytes 4211200 | tf_op jit(solution)/shard_map/thi,hie->the/dot_general | solution.py:28
  117.5 9.7 %all-gather.3 = f32[128,128]{1,0:T(8,128)S(1)} all-gather(f32[16,128]{1,0:T(8,128)S(1)} %bitcast.155), channel_id=5, replica_groups=mesh['dp'=4,'ctx'=8] {'ctx'}, dimensions={0}, use_global_device_ids=true | all-gather | bytes 73728 | tf_op jit(solution)/shard_map/all_gather | solution.py:11
  128.0 2.1 fusion.12
  130.1 2.4 fusion.14
  133.5 2.7 fusion.39
  136.2 27.6 %all-gather.9.cloned.1.call-done = f32[128,128,128]{2,1,0:T(8,128)} async-done(((f32[16,128,128]{2,1,0:T(8,128)}), f32[128,128,128]{2,1,0:T(8,128)}) %all-gather.9.cloned.1.call-update) | async-done | bytes 8388624 | tf_op jit(solution)/shard_map/all_gather | solution.py:11
  163.8 23.7 %while.35 = (s32[]{:T(128)}, f32[16,128,128]{2,1,0:T(8,128)S(1)}, f32[16,128]{1,0:T(8,128)S(1)}, s32[]{:T(128)}, f32[8]{0:T(128)S(1)}, /*index=5*/f32[8,16,128,1...) while((s32[]{:T(128)}, f32[16,128,128]{2,1,0:T(8,128)S(1)}, ...), condition=%wide.region_9.10_spmd.clone, body=%wide.region_8.9_spmd.clone.sunk | while | flops 1056777 | bytes 3170520 | solution.py:24
  165.0 1.7 fusion.73
  168.0 1.7 fusion.73
  187.6 3.0 fusion.10
  192.4 2.5 convolution_convert_fusion.1
  195.9 3.8 %convolution_bitcast_fusion.2 = f32[128,16,128]{0,2,1:T(8,128)S(1)} fusion(f32[16,128,128]{1,2,0:T(8,128)} %get-tuple-element.411, f32[128,16,128]{0,2,1:T(8,128)} %bitcast.145, f32[128,16]{0,1:T(8,128)S(1)} %fusion.37), kind=kOutput, calls=%fused_computation.17 | convolution fusion | flops 402915328 | bytes 3153920 | tf_op jit(solution)/shard_map/hts,the->she/dot_general | solution.py:28
  199.7 4.0 %fusion.20 = bf16[128,16,128]{0,2,1:T(8,128)(2,1)S(1)} fusion(f32[128,16,128]{0,2,1:T(8,128)S(1)} %convolution_bitcast_fusion.2, f32[16,128,128]{2,1,0:T(8,128)S(1)} %get-tuple-element.308, f32[128]{0:T(128)S(1)} %get-tuple-element.400, f32[128,16,128]{2,0,1:T(8,128)} %copy-done.11), kind=kOutput, calls=%fused_computation.40 | convolution fusion | flops 405012480 | bytes 3670528 | tf_op jit(solution)/shard_map/hie,shi->she/dot_general | solution.py:28
  207.0 122.1 %reduce-scatter.2.cloned.1.call-done = f32[64,128]{1,0:T(8,128)} async-done(((f32[2048,128]{1,0:T(8,128)}), f32[64,128]{1,0:T(8,128)}) %reduce-scatter.2.cloned.1.call-update) | async-done | bytes 32784 | tf_op jit(solution)/shard_map/reduce_scatter | solution.py:141
  (119 shorter events, 57.1 us)
Async XLA Ops:
  7.2 8.4 %copy-start = (bf16[16,128,128]{2,1,0:T(8,128)(2,1)S(1)}, bf16[16,128,128]{2,1,0:T(8,128)(2,1)}, u32[]{:S(2)}) copy-start(bf16[16,128,128]{2,1,0:T(8,128)(2,1)} %param.14) | copy-start | bytes 1572868
  7.2 15.3 %copy-start.14 = (u32[32]{0:T(128)S(1)}, u32[32]{0:T(128)}, u32[]{:S(2)}) copy-start(u32[32]{0:T(128)} %constant.117) | copy-start | bytes 388
  7.2 34.5 %copy-start.13 = (bf16[1,128,2048]{2,1,0:T(8,128)(2,1)S(1)}, bf16[1,128,2048]{2,1,0:T(8,128)(2,1)}, u32[]{:S(2)}) copy-start(bf16[1,128,2048]{2,1,0:T(8,128)(2,1)} %param.13) | copy-start | bytes 1572868
  7.2 70.1 %all-gather.7.cloned.1.call-start = ((), (), s32[]{:S(2)}) async-start(), calls=%async_computation.2 | async-start | bytes 9437184 | tf_op jit(solution)/shard_map/all_gather | solution.py:11
  11.7 39.6 %copy-start.6 = (bf16[1,128,2048]{1,2,0:T(8,128)(2,1)}, bf16[1,128,2048]{1,2,0:T(8,128)(2,1)S(1)}, u32[]{:S(2)}) copy-start(bf16[1,128,2048]{1,2,0:T(8,128)(2,1)S(1)} %copy.126) | copy-start | bytes 1572868
  13.1 3.3 copy-start.8
  16.4 1.1 copy-start.11
  20.0 143.8 %all-gather.9.cloned.1.call-start = ((), (), s32[]{:S(2)}) async-start(), calls=%async_computation.3 | async-start | bytes 9437184 | tf_op jit(solution)/shard_map/all_gather | solution.py:11
  51.7 52.9 %copy-start.1 = (f32[128,16,128]{2,0,1:T(8,128)}, f32[128,16,128]{2,0,1:T(8,128)S(1)}, u32[]{:S(2)}) copy-start(f32[128,16,128]{2,0,1:T(8,128)S(1)} %convolution_bitcast_fusion) | copy-start | bytes 3145732
  109.2 219.9 %reduce-scatter.2.cloned.1.call-start = ((), (), s32[]{:S(2)}) async-start(), calls=%async_computation.1 | async-start | bytes 1081344 | tf_op jit(solution)/shard_map/reduce_scatter | solution.py:141
  109.5 6.4 %copy-start.2 = (f32[128,16,128]{2,0,1:T(8,128)S(1)}, f32[128,16,128]{2,0,1:T(8,128)}, u32[]{:S(2)}) copy-start(f32[128,16,128]{2,0,1:T(8,128)} %copy-done.1) | copy-start | bytes 3145732
  109.5 17.7 %copy-start.9 = (bf16[16,8,16,128]{3,2,1,0:T(8,128)(2,1)S(1)}, bf16[16,8,16,128]{3,2,1,0:T(8,128)(2,1)}, u32[]{:S(2)}) copy-start(bf16[16,8,16,128]{3,2,1,0:T(8,128)(2,1)} %copy-done.8) | copy-start | bytes 1572868
  109.5 17.7 %copy-start.10 = (f32[1,128,2048]{1,2,0:T(8,128)S(1)}, f32[1,128,2048]{1,2,0:T(8,128)}, u32[]{:S(2)}) copy-start(f32[1,128,2048]{1,2,0:T(8,128)} %copy.73) | copy-start | bytes 3145732
  111.8 18.3 %copy-start.12 = (f32[128,16,128]{2,0,1:T(8,128)S(1)}, f32[128,16,128]{2,0,1:T(8,128)}, u32[]{:S(2)}) copy-start(f32[128,16,128]{2,0,1:T(8,128)} %copy-done.11) | copy-start | bytes 3145732
  132.5 1.0 copy-start.5
  163.8 26.7 %copy-start.7 = (bf16[1,128,2048]{1,2,0:T(8,128)(2,1)S(1)}, bf16[1,128,2048]{1,2,0:T(8,128)(2,1)}, u32[]{:S(2)}) copy-start(bf16[1,128,2048]{1,2,0:T(8,128)(2,1)} %copy-done.6) | copy-start | bytes 1572868
  190.6 1.7 copy-start.3
  192.3 12.4 %copy-start.4 = (f32[128,16,128]{2,0,1:T(8,128)S(1)}, f32[128,16,128]{2,0,1:T(8,128)}, u32[]{:S(2)}) copy-start(f32[128,16,128]{2,0,1:T(8,128)} %copy-done.3) | copy-start | bytes 3145732
Sparse Core Ops, SparseCore 0:
  20.1 57.1 all-gather.6
  109.3 54.5 all-gather.8
  192.5 136.5 reduce-scatter.1
where the time goes:
time: 337 us; the launch traced here: 336 us
  waiting for transfers between devices  170 us (50%)
  matrix products  49 us (15%)
  blocking collectives  33.9 us (10%)
  other arithmetic  32.5 us (10%)
  local copies, waits for them, and re-layouts  22.9 us (7%)
  between operations  16.6 us (5%)
  loops' own time  10.8 us (3%)
    reduce_scatter x1, waiting for transfers between devices, shards(): lax.psum_scatter(query_term + key_term, ('dp', 'ctx'), scatter_dimension=...  122 us
    dot_general x18, matrix products, einsum_high(): return jnp.einsum(form, *operands, precision=lax.Precision.HIGHEST)  47.8 us
    all_gather x2, waiting for transfers between devices, carried_in(): everything = jax.tree.map(lambda part: lax.all_gather(part, axis), value)  47.4 us
    select_n x32, other arithmetic, step(): return jax.tree.map(lambda a, b: jnp.where(reached, a, b), new, before)  28.1 us
    all_gather x2, blocking collectives, carried_in(): everything = jax.tree.map(lambda part: lax.all_gather(part, axis), value)  18.1 us
    unnamed x1, blocking collectives  15.7 us
    another operation x2, loops' own time, carried_in(): return lax.fori_loop(0, peers, step, start)  10.8 us
    dynamic_slice x16, local copies, waits for them, and re-layouts, step(): new = combine(before, jax.tree.map(lambda part: part[at], everything))  10 us
  transfers between devices with their start and end apart: 3, of which 3 were waited for; matrix products, arithmetic and copies ran while one was open for 13% of the time, Pallas kernels for 0%

commit v1 on v0

v1 whole, which is shorter than its diff:
```python
import functools
import math

import jax
import jax.numpy as jnp
from jax import lax
from jax.experimental import pallas as pl
from jax.experimental.pallas import tpu as pltpu
from jax.sharding import PartitionSpec as P

F32 = jnp.float32
BF16 = jnp.bfloat16
VM = pl.BlockSpec(memory_space=pltpu.VMEM)
SM = pl.BlockSpec(memory_space=pltpu.SMEM)
NN = (((1,), (0,)), ((), ()))
NT = (((1,), (1,)), ((), ()))
TN = (((0,), (0,)), ((), ()))


def split(x):
    hi = x.astype(BF16)
    return hi, (x - hi.astype(F32)).astype(BF16)


def dot(a, b, dims):
    return lax.dot_general(a, b, dims, preferred_element_type=F32)


def cat(parts, axis):
    return jnp.concatenate(parts, axis=axis)


def dot_wide(a, b, dims):
    ka, kb = dims[0][0][0], dims[0][1][0]
    hi, lo = split(a)
    return dot(cat([hi, lo], ka), cat([b, b], kb), dims)


def dot_full(a, b, dims):
    ka, kb = dims[0][0][0], dims[0][1][0]
    ah, al = split(a)
    bh, bl = split(b)
    return dot(cat([ah, al, ah], ka), cat([bh, bh, bl], kb), dims)


def softplus(x):
    return jnp.maximum(x, 0.0) + jnp.log1p(jnp.exp(-jnp.abs(x)))


def sigmoid(x):
    z = jnp.exp(-jnp.abs(x))
    return jnp.where(x >= 0, 1.0, z) / (1.0 + z)


class Docs:
    def __init__(self, lengths_ref, ndoc, rows):
        self.rows = rows
        self.first = (lax.axis_index("ctx") // 2) * rows
        self.starts = [jnp.int32(0)]
        for d in range(ndoc):
            self.starts.append(self.starts[-1] + lengths_ref[0, d])

    def start_of(self, pos):
        out = jnp.zeros_like(pos)
        for s in self.starts[1:]:
            out = jnp.where(pos >= s, s, out)
        return out

    def along(self, axis, shape):
        return self.first + lax.broadcasted_iota(jnp.int32, shape, axis)

    def keep_t(self):
        shape = (self.rows, self.rows)
        s, t = self.along(0, shape), self.along(1, shape)
        begin = self.start_of(self.along(1, (8, self.rows)))[:1]
        return ((s <= t) & (s >= begin)).astype(F32)

    def inside_row(self):
        return (self.start_of(self.along(1, (8, self.rows))) < self.first).astype(F32)[:1]

    def head_row(self):
        begin = self.start_of(self.along(1, (8, self.rows)))
        return (begin <= self.first).astype(F32)[:1]

    def tail_row(self):
        last = self.start_of(self.first + self.rows - 1 + jnp.int32(0))
        return (self.along(1, (8, self.rows)) >= last).astype(F32)[:1]

    def later_col(self, width):
        after = self.start_of(self.first + self.rows + jnp.int32(0))
        return (self.along(0, (self.rows, width)) >= after).astype(F32)


def my_core():
    return lax.rem(lax.axis_index("ctx"), 2)


def place(ref, h, width):
    return ref[:, pl.ds(pl.multiple_of(h * width, width), width)]


def token_pair(own_ref, got_ref, h, nh, width):
    core = my_core()
    own = own_ref[:, pl.ds(pl.multiple_of((core * nh + h) * width, width), width)].astype(F32)
    got = place(got_ref, h, width)
    first = jnp.where(core == 0, own, got)
    second = jnp.where(core == 0, got, own)
    return cat([first, second], 0).astype(BF16)


def key_kernel(nh, ndoc, len_ref, k_ref, v_ref, kg_ref, vg_ref, w_ref,
               fk_ref, fkt_ref, k2_ref, v2_ref, s_ref, n_ref):
    rows, width = fk_ref.shape[1:]
    tail = Docs(len_ref, ndoc, rows).tail_row()
    core = my_core()

    def body(h, _):
        k = token_pair(k_ref, kg_ref, h, nh, width)
        v = token_pair(v_ref, vg_ref, h, nh, width)
        fk = softplus(dot(k, w_ref[core * nh + h], NN))
        fkt = fk.T
        fk_ref[h] = fk
        fkt_ref[h] = fkt
        k2_ref[h] = k
        v2_ref[h] = v
        masked = fkt * tail
        s_ref[h] = dot_wide(masked, v, NN)
        n_ref[h] = jnp.broadcast_to(jnp.sum(masked, axis=1, keepdims=True), (width, 128)).T[:1]
        return 0

    lax.fori_loop(0, nh, body, 0)


def query_kernel(nh, ndoc, len_ref, q_ref, g_ref, qg_ref, gg_ref, w_ref, fk_ref,
                 fqt_ref, sqt_ref, q2_ref, g2_ref, at_ref, dl_ref):
    rows, width = fk_ref.shape[1:]
    keep = Docs(len_ref, ndoc, rows).keep_t()
    core = my_core()

    def body(h, _):
        q = token_pair(q_ref, qg_ref, h, nh, width)
        q2_ref[h] = q
        g2_ref[h] = token_pair(g_ref, gg_ref, h, nh, width)
        pre = dot(q, w_ref[core * nh + h], NN).T
        fqt = softplus(pre)
        fqt_ref[h] = fqt
        sqt_ref[h] = sigmoid(pre)
        at = dot_full(fk_ref[h], fqt, NN) * keep
        at_ref[h] = at
        dl_ref[h] = jnp.sum(at, axis=0, keepdims=True)
        return 0

    lax.fori_loop(0, nh, body, 0)


def rstate_kernel(nh, ndoc, len_ref, fqt_ref, g2_ref, dl_ref, n_ref, inv_ref, r_ref):
    rows = fqt_ref.shape[2]
    docs = Docs(len_ref, ndoc, rows)
    inside, head = docs.inside_row(), docs.head_row()

    def body(h, _):
        fqt = fqt_ref[h]
        norm = jnp.broadcast_to(n_ref[h], (8, n_ref.shape[2]))
        denom = dl_ref[h] + inside * dot_full(norm, fqt, NN)[:1]
        inv = 1.0 / denom
        inv_ref[h] = inv
        r_ref[h] = dot_wide(fqt * (inv * head), g2_ref[h], NN)
        return 0

    lax.fori_loop(0, nh, body, 0)


def fill_kernel(nh, at_ref, inv_ref, g2_ref, v2_ref, k2_ref, w_ref,
                mt_ref, cl_ref, gv_ref, sk_ref):
    core = my_core()

    def body(h, _):
        at = at_ref[h]
        g, v = g2_ref[h], v2_ref[h]
        mt = dot(v, g, NT)
        mt_ref[h] = mt
        cl_ref[h] = jnp.sum(at * mt, axis=0, keepdims=True)
        gv_ref[h] = dot_wide(at * inv_ref[h], g, NN)
        sk_ref[h] = sigmoid(dot(k2_ref[h], w_ref[core * nh + h], NN))
        return 0

    lax.fori_loop(0, nh, body, 0)


def out_pair(x, own_ref, send_ref, h, width):
    core = my_core()
    half = x.shape[0] // 2
    own = jnp.where(core == 0, x[:half], x[half:])
    other = jnp.where(core == 0, x[half:], x[:half])
    at = pl.ds(pl.multiple_of(h * width, width), width)
    own_ref[:, at] = own.astype(BF16)
    send_ref[:, at] = other


def forward_kernel(nh, ndoc, len_ref, s_ref, n_ref, mt_ref, cl_ref, inv_ref, g2_ref, q2_ref,
                   fqt_ref, sqt_ref, fk_ref, fkt_ref, w_ref,
                   gq_ref, gqs_ref, qt_ref, rn_ref, gfk_ref):
    rows, width = fk_ref.shape[1:]
    docs = Docs(len_ref, ndoc, rows)
    keep, inside, head = docs.keep_t(), docs.inside_row(), docs.head_row()
    core = my_core()

    def body(h, _):
        w = w_ref[core * nh + h]
        fqt, inv = fqt_ref[h], inv_ref[h]
        ut = dot_wide(s_ref[h], g2_ref[h], NT)
        c = (cl_ref[h] + inside * jnp.sum(fqt * ut, axis=0, keepdims=True)) * inv
        shift = -c * inv
        rn_ref[h] = dot_full(jnp.broadcast_to(shift * head, (8, rows)), fqt, NT)[:1]
        pt = (mt_ref[h] - c) * inv * keep
        gfk_ref[h] = dot_full(pt, fqt, NT)
        norm = jnp.broadcast_to(n_ref[h], (width, width)).T
        carried = ut * inv + cat([norm] * (rows // width), 1) * shift
        gfq = dot_full(fkt_ref[h], pt, NN) + inside * carried
        gpq = gfq * sqt_ref[h]
        hi, lo = split(gpq)
        gq = dot(cat([w, w], 1), cat([hi, lo], 0), NN).T
        out_pair(gq, gq_ref, gqs_ref, h, width)
        q = q2_ref[h]
        qt_ref[h] = dot(cat([hi, lo], 1), cat([q, q], 0), NN).T
        return 0

    lax.fori_loop(0, nh, body, 0)


def backward_kernel(nh, ndoc, factor, len_ref, r_ref, rn_ref, gfk_ref, gv0_ref, sk_ref, fk_ref,
                    k2_ref, v2_ref, qt_ref, w_ref,
                    wt_ref, gk_ref, gks_ref, gv_ref, gvs_ref):
    rows, width = fk_ref.shape[1:]
    later = Docs(len_ref, ndoc, rows).later_col(width)
    core = my_core()

    def body(h, _):
        w = w_ref[core * nh + h]
        r = r_ref[h]
        rh, rl = split(r)
        v = v2_ref[h]
        carried = dot(cat([v, v], 1), cat([rh, rl], 1), NT) + rn_ref[h]
        gpk = (gfk_ref[h] + later * carried) * sk_ref[h]
        hi, lo = split(gpk)
        k = k2_ref[h]
        wt_ref[h] = (dot(cat([k, k], 0), cat([hi, lo], 0), TN) + qt_ref[h]) * factor
        out_pair(dot(cat([hi, lo], 1), cat([w, w], 1), NT), gk_ref, gks_ref, h, width)
        fh, fl = split(fk_ref[h])
        gv = gv0_ref[h] + later * dot(cat([fh, fl, fh], 1), cat([rh, rh, rl], 0), NN)
        out_pair(gv, gv_ref, gvs_ref, h, width)
        return 0

    lax.fori_loop(0, nh, body, 0)


def join_kernel(own_ref, got_ref, out_ref):
    core = my_core()
    half = own_ref.shape[1]
    out_ref[:, pl.ds(pl.multiple_of(core * half, half), half)] = own_ref[...]
    out_ref[:, pl.ds(pl.multiple_of((1 - core) * half, half), half)] = got_ref[...].astype(BF16)


def call(kernel, outs, name, smem=0, limit=24 << 20):
    def run(*args):
        return pl.pallas_call(
            kernel,
            out_shape=[jax.ShapeDtypeStruct(s, d) for s, d in outs],
            in_specs=[SM] * smem + [VM] * (len(args) - smem),
            out_specs=[VM] * len(outs),
            compiler_params=pltpu.CompilerParams(vmem_limit_bytes=limit),
            name=name,
        )(*args)

    return run


def shards(queries, keys, values, out_grad, feature_weight, doc_lengths):
    ctx = lax.axis_size("ctx")
    dp = lax.axis_size("dp")
    tok = queries.shape[1]
    heads, width, _ = feature_weight.shape
    ndoc = doc_lengths.shape[1]
    chips = ctx // 2
    nh = heads // 2
    rows = 2 * tok
    here = lax.axis_index("ctx")
    core = here % 2
    chip = here // 2
    longest = ctx * tok // 4
    hops = -(-longest // rows)
    factor = 1.0 / math.sqrt(dp * ctx * tok)

    swap = [(i, i ^ 1) for i in range(ctx)]
    ahead = [(i, i + 2) for i in range(ctx - 2)]
    back = [(i + 2, i) for i in range(ctx - 2)]

    def other_half(x):
        part = lax.dynamic_slice_in_dim(x, (1 - core) * nh * width, nh * width, axis=1)
        return lax.ppermute(part.astype(F32), "ctx", swap)

    q, k, v, g = queries[0], keys[0], values[0], out_grad[0]
    kg, vg = other_half(k), other_half(v)
    qg, gg = other_half(q), other_half(g)
    w = feature_weight

    if hops > 1:
        ends = jnp.cumsum(doc_lengths[0])
        begins = jnp.concatenate([jnp.zeros((1,), jnp.int32), ends])

        def start_of(p):
            return jnp.max(jnp.where(begins <= p, begins, 0))

    def carry(x, forward):
        total = moved = lax.ppermute(x, "ctx", ahead if forward else back)
        for h in range(1, hops):
            moved = lax.ppermute(moved, "ctx", ahead if forward else back)
            if forward:
                gate = start_of(chip * rows) < (chip - h) * rows
            else:
                gate = start_of((chip + 1 + h) * rows) < (chip + 1) * rows
            total = total + jnp.where(gate, moved, 0.0)
        return total

    wide = (nh, rows, width)
    tall = (nh, width, rows)
    square = (nh, rows, rows)
    state = (nh, width, width)
    norm = (nh, 1, width)
    line = (nh, 1, rows)
    half = (tok, nh * width)

    fk, fkt, k2, v2, s_loc, n_loc = call(
        functools.partial(key_kernel, nh, ndoc),
        [(wide, F32), (tall, F32), (wide, BF16), (wide, BF16), (state, F32), (norm, F32)],
        "key", 1,
    )(doc_lengths, k, v, kg, vg, w)
    n_in = carry(n_loc, True)
    s_in = carry(s_loc, True)
    fqt, sqt, q2, g2, at, dl = call(
        functools.partial(query_kernel, nh, ndoc),
        [(tall, F32), (tall, F32), (wide, BF16), (wide, BF16), (square, F32), (line, F32)],
        "query", 1,
    )(doc_lengths, q, g, qg, gg, w, fk)
    inv, r_loc = call(
        functools.partial(rstate_kernel, nh, ndoc), [(line, F32), (state, F32)], "rstate", 1
    )(doc_lengths, fqt, g2, dl, n_in)
    r_in = carry(r_loc, False)
    mt, cl, gv0, sk = call(
        functools.partial(fill_kernel, nh),
        [(square, F32), (line, F32), (wide, F32), (wide, F32)],
        "fill",
    )(at, inv, g2, v2, k2, w)
    gq, gqs, qt, rn, gfk = call(
        functools.partial(forward_kernel, nh, ndoc),
        [(half, BF16), (half, F32), (state, F32), (norm, F32), (wide, F32)],
        "forward", 1,
    )(doc_lengths, s_in, n_in, mt, cl, inv, g2, q2, fqt, sqt, fk, fkt, w)
    rn_in = carry(rn, False)
    gqg = lax.ppermute(gqs, "ctx", swap)
    wt, gk, gks, gv, gvs = call(
        functools.partial(backward_kernel, nh, ndoc, factor),
        [(state, F32), (half, BF16), (half, F32), (half, BF16), (half, F32)],
        "backward", 1,
    )(doc_lengths, r_in, rn_in, gfk, gv0, sk, fk, k2, v2, qt, w)

    each = heads * width // (dp * ctx)
    wt = wt.reshape(dp // 2, chips, 2 * each, width)

    def block(to):
        return lax.dynamic_index_in_dim(wt, to, axis=1, keepdims=False)

    total = block(chip)
    moved = []
    for j in range(1, chips):
        perm = [(i, ((i // 2) ^ j) * 2 + i % 2) for i in range(ctx)]
        moved.append(lax.ppermute(block(chip ^ j), "ctx", perm))
    for part in moved:
        total = total + part
    total = total.reshape(dp, each, width)
    z = lax.axis_index("dp")
    moved = []
    for r in range(dp):
        perm = []
        for zz in range(dp):
            for i in range(ctx):
                to = (i % 2) * (dp // 2) + ((zz ^ r) >> 1)
                perm.append((zz * ctx + i, to * ctx + (i // 2) * 2 + ((zz ^ r) & 1)))
        part = lax.dynamic_index_in_dim(total, z ^ r, axis=0, keepdims=False)
        moved.append(lax.ppermute(part, ("dp", "ctx"), perm))
    grad_weight = functools.reduce(jnp.add, moved)

    gkg = lax.ppermute(gks, "ctx", swap)
    gvg = lax.ppermute(gvs, "ctx", swap)

    def join(own, got):
        return call(join_kernel, [((tok, heads * width), BF16)], "join")(own, got)[0][None]

    return (join(gq, gqg), join(gk, gkg), join(gv, gvg), grad_weight)


def solution(mesh):
    placed = (
        P("dp", "ctx", None),
        P("dp", "ctx", None),
        P("dp", "ctx", None),
        P("dp", "ctx", None),
        P(),
        P("dp", None),
    )
    return jax.shard_map(
        shards,
        mesh=mesh,
        in_specs=placed,
        out_specs=(
            P("dp", "ctx", None),
            P("dp", "ctx", None),
            P("dp", "ctx", None),
            P(("dp", "ctx"), None),
        ),
        check_vma=False,
    )
```

time: 337 us -> 92.2 us (0.27)
  waiting for transfers between devices: 170 us -> 17.6 us
  matrix products: 49 us -> 0 us
  blocking collectives: 33.9 us -> 0 us
  Pallas kernels: 0 us -> 30.1 us
  other arithmetic: 32.5 us -> 4.79 us
  starting transfers between devices: 0.34 us -> 27.4 us
  between operations: 16.6 us -> 0.97 us
  local copies, waits for them, and re-layouts: 22.9 us -> 10.9 us
  loops' own time: 10.8 us -> 0 us
    reduce_scatter x1 -> x0, waiting for transfers between devices: 122 us -> none  [shards(): lax.psum_scatter(query_term + key_term, ('dp', 'ctx'), scatter_dimension=...]
    dot_general x20 -> x0, matrix products: 49 us -> none  [the longest x18 47.8 us: einsum_high(): return jnp.einsum(form, *operands, precision=lax.Precision.HIGHEST)]
    all_gather x2 -> x0, waiting for transfers between devices: 47.4 us -> none  [carried_in(): everything = jax.tree.map(lambda part: lax.all_gather(part, axis), value)]
    pallas_call x0 -> x9, Pallas kernels: none -> 30.1 us  [run(): pl.pallas_call(kernel, out_shape=[jax.ShapeDtypeStruct(s, d) for s, d in...]
    select_n x32 -> x0, other arithmetic: 28.1 us -> none  [step(): return jax.tree.map(lambda a, b: jnp.where(reached, a, b), new, before)]
    ppermute x0 -> x18, starting transfers between devices: none -> 27.4 us  [the longest x4 10.7 us: carry(): total = moved = lax.ppermute(x, 'ctx', ahead if forward else back)]
    all_gather x2 -> x0, blocking collectives: 18.1 us -> none  [carried_in(): everything = jax.tree.map(lambda part: lax.all_gather(part, axis), value)]
    ppermute x0 -> x18, waiting for transfers between devices: none -> 17.6 us  [the longest x4 8.51 us: carry(): total = moved = lax.ppermute(x, 'ctx', ahead if forward else back)]
  transfers between devices with their start and end apart: 3 -> 18, of which waited for: 3 -> 8; matrix products, arithmetic and copies ran while one was open for 13% -> 4% of each run, Pallas kernels for 0% -> 27%
where the time goes in v1:
time: 92.2 us; the launch traced here: 91.7 us
  Pallas kernels  30.1 us (33%)
  starting transfers between devices  27.4 us (30%)
  waiting for transfers between devices  17.6 us (19%)
  local copies, waits for them, and re-layouts  10.9 us (12%)
  other arithmetic  4.79 us (5%)
  between operations  0.97 us (1%)
    pallas_call x9, Pallas kernels, run(): pl.pallas_call(kernel, out_shape=[jax.ShapeDtypeStruct(s, d) for s, d in...  30.1 us
    unnamed x46, local copies, waits for them, and re-layouts  10.9 us
    ppermute x4, starting transfers between devices, carry(): total = moved = lax.ppermute(x, 'ctx', ahead if forward else back)  10.7 us
    ppermute x4, starting transfers between devices, shards(): moved.append(lax.ppermute(part, ('dp', 'ctx'), perm))  9.98 us
    ppermute x4, waiting for transfers between devices, carry(): total = moved = lax.ppermute(x, 'ctx', ahead if forward else back)  8.51 us
    ppermute x4, waiting for transfers between devices, shards(): moved.append(lax.ppermute(part, ('dp', 'ctx'), perm))  4.99 us
    ppermute x3, starting transfers between devices, shards(): moved.append(lax.ppermute(block(chip ^ j), 'ctx', perm))  4.93 us
    ppermute x3, waiting for transfers between devices, shards(): moved.append(lax.ppermute(block(chip ^ j), 'ctx', perm))  3.94 us
  transfers between devices with their start and end apart: 18, of which 8 were waited for; matrix products, arithmetic and copies ran while one was open for 4% of the time, Pallas kernels for 27%

profile of v1, /device:TPU:0, one launch (start us, length us, event | category | flops | bytes accessed | tf_op | source)
XLA Modules:
  0.0 91.7 jit_solution(3500311720614139968)
XLA Ops:
  0.7 1.1 %bitcast_convert_fusion.3 = f32[128,1024]{1,0:T(8,128)S(1)} fusion(bf16[1,128,2048]{2,1,0:T(8,128)(2,1)} %param.7, s32[]{:T(128)S(6)} %select_n.44), kind=kLoop, calls=%fused_computation.3 | loop fusion | flops 131072 | bytes 786436 | tf_op jit(solution)/shard_map/convert_element_type | solution.py:300
  5.4 3.9 %key.1 = (f32[8,256,128]{2,1,0:T(8,128)S(1)}, f32[8,128,256]{2,1,0:T(8,128)S(1)}, bf16[8,256,128]{2,1,0:T(8,128)(2,1)S(1)}, bf16[8,256,128]{2,1,0:T(8,128)(2,1)S...) custom-call(s32[1,8]{1,0:T(1,128)S(1)} %copy-done.19, bf16[128,2048]{1,0:T(8,128)(2,1)S(1)} %bitcast.41, ...), custom_call_target="tpu_custom_call" | custom-call | tf_op jit(solution)/shard_map/key/pallas_call | solution.py:266
  9.3 4.7 %collective-permute-start.2 = (f32[8,128,128]{2,1,0:T(8,128)S(1)}, f32[8,128,128]{2,1,0:T(8,128)S(1)}, u32[]{:S(2)}, u32[]{:S(2)}) collective-permute-start(f32[8,128,128]{2,1,0:T(8,128)S(1)} %get-tuple-element.32), channel_id=1, source_target_pairs={{0,2},{1,3},{2,4},{3,5},{4,6},{5,7},{8,10},{9,11},{10,12},{11,13},... | collective-permute-start | bytes 1572872 | tf_op jit(solution)/shard_map/ppermute | solution.py:315
  14.0 3.4 %collective-permute-start.3 = (f32[8,1,128]{2,1,0:T(1,128)S(1)}, f32[8,1,128]{2,1,0:T(1,128)S(1)}, u32[]{:S(2)}, u32[]{:S(2)}) collective-permute-start(f32[8,1,128]{2,1,0:T(1,128)S(1)} %get-tuple-element.33), channel_id=1, source_target_pairs={{0,2},{1,3},{2,4},{3,5},{4,6},{5,7},{8,10},{9,11},{10,12},{11,13},... | collective-permute-start | bytes 12296 | tf_op jit(solution)/shard_map/ppermute | solution.py:315
  17.4 4.9 %query.1 = (f32[8,128,256]{2,1,0:T(8,128)S(1)}, f32[8,128,256]{2,1,0:T(8,128)S(1)}, bf16[8,256,128]{2,1,0:T(8,128)(2,1)S(1)}, bf16[8,256,128]{2,1,0:T(8,128)(2,1...) custom-call(s32[1,8]{1,0:T(1,128)S(1)} %copy-done.19, bf16[128,2048]{1,0:T(8,128)(2,1)S(1)} %bitcast.43, ...), custom_call_target="tpu_custom_call" | custom-call | tf_op jit(solution)/shard_map/query/pallas_call | solution.py:266
  22.4 3.2 %collective-permute-done.3.n_ref = f32[8,1,128]{2,1,0:T(1,128)S(1)} collective-permute-done((f32[8,1,128]{2,1,0:T(1,128)S(1)}, f32[8,1,128]{2,1,0:T(1,128)S(1)}, u32[]{:S(2)}, u32[]{:S(2)}) %collective-permute-start.3) | collective-permute-done | bytes 4128 | tf_op jit(solution)/shard_map/ppermute | solution.py:315
  25.6 4.3 %rstate.1 = (f32[8,1,256]{2,1,0:T(1,128)S(1)}, f32[8,128,128]{2,1,0:T(8,128)}) custom-call(s32[1,8]{1,0:T(1,128)S(1)} %copy-done.19, f32[8,128,256]{2,1,0:T(8,128)S(1)} %get-tuple-element.36.fqt_ref, bf16[8,256,128]{2,1,0:T(8,128)(2,1)S(1)} %get-tuple-element.37.g2_ref, f32[8,1,256]{2,1,0:T(1,128)S(1)} %get-tuple-element.38.dl_ref, ...), custom_call_target="tpu_custom_call" | custom-call | tf_op jit(solution)/shard_map/rstate/pallas_call | solution.py:266
  29.9 1.3 %collective-permute-start.7 = (f32[8,128,128]{2,1,0:T(8,128)}, f32[8,128,128]{2,1,0:T(8,128)S(1)}, u32[]{:S(2)}, u32[]{:S(2)}) collective-permute-start(f32[8,128,128]{2,1,0:T(8,128)} %get-tuple-element.49), channel_id=1, source_target_pairs={{2,0},{3,1},{4,2},{5,3},{6,4},{7,5},{10,8},{11,9},{12,10},{13,11},... | collective-permute-start | bytes 1572872 | tf_op jit(solution)/shard_map/ppermute | solution.py:315
  31.2 2.3 %fill.1 = (f32[8,256,256]{2,1,0:T(8,128)S(1)}, f32[8,1,256]{2,1,0:T(1,128)S(1)}, f32[8,256,128]{2,1,0:T(8,128)S(1)}, f32[8,256,128]{2,1,0:T(8,128)S(1)}) custom-call(f32[8,256,256]{2,1,0:T(8,128)S(1)} %get-tuple-element.35.at_ref, f32[8,1,256]{2,1,0:T(1,128)S(1)} %get-tuple-element.39.inv_ref, bf16[8,256,128]{2,1,0:T(8,128)(2,1)S(1)} %get-tuple-element.37.g2_ref, ...), custom_call_target="tpu_custom_call" | custom-call | tf_op jit(solution)/shard_map/fill/pallas_call | solution.py:266
  34.5 7.5 %forward.1 = (bf16[128,1024]{1,0:T(8,128)(2,1)S(1)}, f32[128,1024]{1,0:T(8,128)S(1)}, f32[8,128,128]{2,1,0:T(8,128)S(1)}, f32[8,1,128]{2,1,0:T(1,128)S(1)}, f32[8,256,128]{2,1,0:T(8,128)S(1)}) custom-call(s32[1,8]{1,0:T(1,128)S(1)} %copy-done.19, f32[8,128,128]{2,1,0:T(8,128)S(1)} %collective-permute-done.2.s_ref, ...), custom_call_target="tpu_custom_call" | custom-call | tf_op jit(solution)/shard_map/forward/pallas_call | solution.py:266
  44.6 1.3 %collective-permute-start.8 = (f32[8,1,128]{2,1,0:T(1,128)S(1)}, f32[8,1,128]{2,1,0:T(1,128)S(1)}, u32[]{:S(2)}, u32[]{:S(2)}) collective-permute-start(f32[8,1,128]{2,1,0:T(1,128)S(1)} %get-tuple-element.50), channel_id=1, source_target_pairs={{2,0},{3,1},{4,2},{5,3},{6,4},{7,5},{10,8},{11,9},{12,10},{13,11},... | collective-permute-start | bytes 12296 | tf_op jit(solution)/shard_map/ppermute | solution.py:315
  45.9 5.3 %collective-permute-done.8.rn_ref = f32[8,1,128]{2,1,0:T(1,128)S(1)} collective-permute-done((f32[8,1,128]{2,1,0:T(1,128)S(1)}, f32[8,1,128]{2,1,0:T(1,128)S(1)}, u32[]{:S(2)}, u32[]{:S(2)}) %collective-permute-start.8) | collective-permute-done | bytes 4128 | tf_op jit(solution)/shard_map/ppermute | solution.py:315
  51.2 1.2 %copy-done.7 = f32[8,256,128]{2,1,0:T(8,128)S(1)} copy-done((f32[8,256,128]{2,1,0:T(8,128)S(1)}, f32[8,256,128]{2,1,0:T(8,128)}, u32[]{:S(2)}) %copy-start.7) | copy-done | bytes 1048600
  52.4 1.2 %copy-done.9 = f32[8,256,128]{2,1,0:T(8,128)S(1)} copy-done((f32[8,256,128]{2,1,0:T(8,128)S(1)}, f32[8,256,128]{2,1,0:T(8,128)}, u32[]{:S(2)}) %copy-start.9) | copy-done | bytes 1048600
  53.7 1.2 %copy-done.11 = f32[8,256,128]{2,1,0:T(8,128)S(1)} copy-done((f32[8,256,128]{2,1,0:T(8,128)S(1)}, f32[8,256,128]{2,1,0:T(8,128)}, u32[]{:S(2)}) %copy-start.11) | copy-done | bytes 1048600
  55.9 4.7 %backward.1 = (f32[8,128,128]{2,1,0:T(8,128)S(1)}, bf16[128,1024]{1,0:T(8,128)(2,1)S(1)}, f32[128,1024]{1,0:T(8,128)S(1)}, bf16[128,1024]{1,0:T(8,128)(2,1)S(1)}, f32[128,1024]{1,0:T(8,128)S(1)}) custom-call(s32[1,8]{1,0:T(1,128)S(1)} %copy-done.19, f32[8,128,128]{2,1,0:T(8,128)S(1)} %collective-permute-done.7.r_ref, ...), custom_call_target="tpu_custom_call" | custom-call | tf_op jit(solution)/shard_map/backward/pallas_call | solution.py:266
  63.2 2.9 %collective-permute-start.11 = (f32[2,128,128]{2,1,0:T(8,128)S(1)}, f32[2,128,128]{2,1,0:T(8,128)S(1)}, u32[]{:S(2)}, u32[]{:S(2)}) collective-permute-start(f32[2,128,128]{2,1,0:T(8,128)S(1)} %get-tuple-element.60), channel_id=1, source_target_pairs={{0,2},{1,3},{2,0},{3,1},{4,6},{5,7},{6,4},{7,5},{8,10},{9,11},{10,... | collective-permute-start | bytes 393224 | tf_op jit(solution)/shard_map/ppermute | solution.py:377
  66.7 1.4 %collective-permute-start.13 = (f32[2,128,128]{2,1,0:T(8,128)S(1)}, f32[2,128,128]{2,1,0:T(8,128)S(1)}, u32[]{:S(2)}, u32[]{:S(2)}) collective-permute-start(f32[2,128,128]{2,1,0:T(8,128)S(1)} %get-tuple-element.61), channel_id=1, source_target_pairs={{0,6},{1,7},{2,4},{3,5},{4,2},{5,3},{6,0},{7,1},{8,14},{9,15},{10,... | collective-permute-start | bytes 393224 | tf_op jit(solution)/shard_map/ppermute | solution.py:377
  68.6 1.7 %collective-permute-done.11 = f32[2,128,128]{2,1,0:T(8,128)S(1)} collective-permute-done((f32[2,128,128]{2,1,0:T(8,128)S(1)}, f32[2,128,128]{2,1,0:T(8,128)S(1)}, u32[]{:S(2)}, u32[]{:S(2)}) %collective-permute-start.11) | collective-permute-done | bytes 131104 | tf_op jit(solution)/shard_map/ppermute | solution.py:377
  71.1 1.5 %collective-permute-done.13 = f32[2,128,128]{2,1,0:T(8,128)S(1)} collective-permute-done((f32[2,128,128]{2,1,0:T(8,128)S(1)}, f32[2,128,128]{2,1,0:T(8,128)S(1)}, u32[]{:S(2)}, u32[]{:S(2)}) %collective-permute-start.13) | collective-permute-done | bytes 131104 | tf_op jit(solution)/shard_map/ppermute | solution.py:377
  74.2 4.0 %collective-permute-start.15 = (f32[64,128]{1,0:T(8,128)S(1)}, f32[64,128]{1,0:T(8,128)S(1)}, u32[]{:S(2)}, u32[]{:S(2)}) collective-permute-start(f32[64,128]{1,0:T(8,128)S(1)} %get-tuple-element.63), channel_id=1, source_target_pairs={{0,1},{1,17},{2,3},{3,19},{4,5},{5,21},{6,7},{7,23},{8,0},{9,16},{... | collective-permute-start | bytes 98312 | tf_op jit(solution)/shard_map/ppermute | solution.py:390
  78.2 2.7 %collective-permute-start.16 = (f32[64,128]{1,0:T(8,128)S(1)}, f32[64,128]{1,0:T(8,128)S(1)}, u32[]{:S(2)}, u32[]{:S(2)}) collective-permute-start(f32[64,128]{1,0:T(8,128)S(1)} %get-tuple-element.65), channel_id=1, source_target_pairs={{0,8},{1,24},{2,10},{3,26},{4,12},{5,28},{6,14},{7,30},{8,9},{9,25... | collective-permute-start | bytes 98312 | tf_op jit(solution)/shard_map/ppermute | solution.py:390
  80.9 2.6 %collective-permute-start.17 = (f32[64,128]{1,0:T(8,128)S(1)}, f32[64,128]{1,0:T(8,128)S(1)}, u32[]{:S(2)}, u32[]{:S(2)}) collective-permute-start(f32[64,128]{1,0:T(8,128)S(1)} %get-tuple-element.64), channel_id=1, source_target_pairs={{0,9},{1,25},{2,11},{3,27},{4,13},{5,29},{6,15},{7,31},{8,8},{9,24... | collective-permute-start | bytes 98312 | tf_op jit(solution)/shard_map/ppermute | solution.py:390
  84.2 4.4 %collective-permute-done.17 = f32[64,128]{1,0:T(8,128)S(1)} collective-permute-done((f32[64,128]{1,0:T(8,128)S(1)}, f32[64,128]{1,0:T(8,128)S(1)}, u32[]{:S(2)}, u32[]{:S(2)}) %collective-permute-start.17) | collective-permute-done | bytes 32800 | tf_op jit(solution)/shard_map/ppermute | solution.py:390
  (75 shorter events, 18.0 us)
Async XLA Ops:
  0.6 4.8 %copy-start.1 = (bf16[1,128,2048]{2,1,0:T(8,128)(2,1)S(1)}, bf16[1,128,2048]{2,1,0:T(8,128)(2,1)}, u32[]{:S(2)}) copy-start(bf16[1,128,2048]{2,1,0:T(8,128)(2,1)} %param.7) | copy-start | bytes 1572868
  1.8 3.4 %collective-permute-start = (f32[128,1024]{1,0:T(8,128)S(1)}, f32[128,1024]{1,0:T(8,128)S(1)}, u32[]{:S(2)}, u32[]{:S(2)}) collective-permute-start(f32[128,1024]{1,0:T(8,128)S(1)} %bitcast_convert_fusion.3), channel_id=1, source_target_pairs={{0,1},{1,0},{2,3},{3,2},{4,5},{5,4},{6,7},{7,6},{8,9},{9,8},{10,11... | collective-permute-start | bytes 1572872 | tf_op jit(solution)/shard_map/ppermute | solution.py:300
  3.4 14.0 %copy-start.3 = (bf16[1,128,2048]{2,1,0:T(8,128)(2,1)S(1)}, bf16[1,128,2048]{2,1,0:T(8,128)(2,1)}, u32[]{:S(2)}) copy-start(bf16[1,128,2048]{2,1,0:T(8,128)(2,1)} %param.6) | copy-start | bytes 1572868
  3.4 14.0 %copy-start.5 = (bf16[1,128,2048]{2,1,0:T(8,128)(2,1)S(1)}, bf16[1,128,2048]{2,1,0:T(8,128)(2,1)}, u32[]{:S(2)}) copy-start(bf16[1,128,2048]{2,1,0:T(8,128)(2,1)} %param.9) | copy-start | bytes 1572868
  3.4 2.0 %collective-permute-start.1 = (f32[128,1024]{1,0:T(8,128)S(1)}, f32[128,1024]{1,0:T(8,128)S(1)}, u32[]{:S(2)}, u32[]{:S(2)}) collective-permute-start(f32[128,1024]{1,0:T(8,128)S(1)} %bitcast_convert_fusion.2), channel_id=1, source_target_pairs={{0,1},{1,0},{2,3},{3,2},{4,5},{5,4},{6,7},{7,6},{8,9},{9,8},{10,11... | collective-permute-start | bytes 1572872 | tf_op jit(solution)/shard_map/ppermute | solution.py:300
  4.6 12.8 %collective-permute-start.4 = (f32[128,1024]{1,0:T(8,128)S(1)}, f32[128,1024]{1,0:T(8,128)S(1)}, u32[]{:S(2)}, u32[]{:S(2)}) collective-permute-start(f32[128,1024]{1,0:T(8,128)S(1)} %bitcast_convert_fusion.1), channel_id=1, source_target_pairs={{0,1},{1,0},{2,3},{3,2},{4,5},{5,4},{6,7},{7,6},{8,9},{9,8},{10,11... | collective-permute-start | bytes 1572872 | tf_op jit(solution)/shard_map/ppermute | solution.py:300
  5.1 12.3 %collective-permute-start.5 = (f32[128,1024]{1,0:T(8,128)S(1)}, f32[128,1024]{1,0:T(8,128)S(1)}, u32[]{:S(2)}, u32[]{:S(2)}) collective-permute-start(f32[128,1024]{1,0:T(8,128)S(1)} %bitcast_convert_fusion), channel_id=1, source_target_pairs={{0,1},{1,0},{2,3},{3,2},{4,5},{5,4},{6,7},{7,6},{8,9},{9,8},{10,11... | collective-permute-start | bytes 1572872 | tf_op jit(solution)/shard_map/ppermute | solution.py:300
  9.3 25.2 %collective-permute-start.2 = (f32[8,128,128]{2,1,0:T(8,128)S(1)}, f32[8,128,128]{2,1,0:T(8,128)S(1)}, u32[]{:S(2)}, u32[]{:S(2)}) collective-permute-start(f32[8,128,128]{2,1,0:T(8,128)S(1)} %get-tuple-element.32), channel_id=1, source_target_pairs={{0,2},{1,3},{2,4},{3,5},{4,6},{5,7},{8,10},{9,11},{10,12},{11,13},... | collective-permute-start | bytes 1572872 | tf_op jit(solution)/shard_map/ppermute | solution.py:315
  14.0 11.6 %collective-permute-start.3 = (f32[8,1,128]{2,1,0:T(1,128)S(1)}, f32[8,1,128]{2,1,0:T(1,128)S(1)}, u32[]{:S(2)}, u32[]{:S(2)}) collective-permute-start(f32[8,1,128]{2,1,0:T(1,128)S(1)} %get-tuple-element.33), channel_id=1, source_target_pairs={{0,2},{1,3},{2,4},{3,5},{4,6},{5,7},{8,10},{9,11},{10,12},{11,13},... | collective-permute-start | bytes 12296 | tf_op jit(solution)/shard_map/ppermute | solution.py:315
  29.9 21.3 %collective-permute-start.7 = (f32[8,128,128]{2,1,0:T(8,128)}, f32[8,128,128]{2,1,0:T(8,128)S(1)}, u32[]{:S(2)}, u32[]{:S(2)}) collective-permute-start(f32[8,128,128]{2,1,0:T(8,128)} %get-tuple-element.49), channel_id=1, source_target_pairs={{2,0},{3,1},{4,2},{5,3},{6,4},{7,5},{10,8},{11,9},{12,10},{13,11},... | collective-permute-start | bytes 1572872 | tf_op jit(solution)/shard_map/ppermute | solution.py:315
  34.5 7.5 %copy-start.6 = (f32[8,256,128]{2,1,0:T(8,128)}, f32[8,256,128]{2,1,0:T(8,128)S(1)}, u32[]{:S(2)}) copy-start(f32[8,256,128]{2,1,0:T(8,128)S(1)} %get-tuple-element.52.gv0_ref) | copy-start | bytes 3145732
  44.6 6.6 %collective-permute-start.8 = (f32[8,1,128]{2,1,0:T(1,128)S(1)}, f32[8,1,128]{2,1,0:T(1,128)S(1)}, u32[]{:S(2)}, u32[]{:S(2)}) collective-permute-start(f32[8,1,128]{2,1,0:T(1,128)S(1)} %get-tuple-element.50), channel_id=1, source_target_pairs={{2,0},{3,1},{4,2},{5,3},{6,4},{7,5},{10,8},{11,9},{12,10},{13,11},... | collective-permute-start | bytes 12296 | tf_op jit(solution)/shard_map/ppermute | solution.py:315
  63.2 27.7 %copy-start.16 = (bf16[128,1024]{1,0:T(8,128)(2,1)S(1)}, bf16[128,1024]{1,0:T(8,128)(2,1)}, u32[]{:S(2)}) copy-start(bf16[128,1024]{1,0:T(8,128)(2,1)} %copy-done.15) | copy-start | bytes 786436
  63.2 7.1 %collective-permute-start.11 = (f32[2,128,128]{2,1,0:T(8,128)S(1)}, f32[2,128,128]{2,1,0:T(8,128)S(1)}, u32[]{:S(2)}, u32[]{:S(2)}) collective-permute-start(f32[2,128,128]{2,1,0:T(8,128)S(1)} %get-tuple-element.60), channel_id=1, source_target_pairs={{0,2},{1,3},{2,0},{3,1},{4,6},{5,7},{6,4},{7,5},{8,10},{9,11},{10,... | collective-permute-start | bytes 393224 | tf_op jit(solution)/shard_map/ppermute | solution.py:377
  66.1 23.9 %copy-start.18 = (bf16[128,1024]{1,0:T(8,128)(2,1)S(1)}, bf16[128,1024]{1,0:T(8,128)(2,1)}, u32[]{:S(2)}) copy-start(bf16[128,1024]{1,0:T(8,128)(2,1)} %copy-done.17) | copy-start | bytes 786436
  66.1 5.0 %collective-permute-start.12 = (f32[2,128,128]{2,1,0:T(8,128)S(1)}, f32[2,128,128]{2,1,0:T(8,128)S(1)}, u32[]{:S(2)}, u32[]{:S(2)}) collective-permute-start(f32[2,128,128]{2,1,0:T(8,128)S(1)} %get-tuple-element.62), channel_id=1, source_target_pairs={{0,4},{1,5},{2,6},{3,7},{4,0},{5,1},{6,2},{7,3},{8,12},{9,13},{10,... | collective-permute-start | bytes 393224 | tf_op jit(solution)/shard_map/ppermute | solution.py:377
  66.7 5.9 %collective-permute-start.13 = (f32[2,128,128]{2,1,0:T(8,128)S(1)}, f32[2,128,128]{2,1,0:T(8,128)S(1)}, u32[]{:S(2)}, u32[]{:S(2)}) collective-permute-start(f32[2,128,128]{2,1,0:T(8,128)S(1)} %get-tuple-element.61), channel_id=1, source_target_pairs={{0,6},{1,7},{2,4},{3,5},{4,2},{5,3},{6,0},{7,1},{8,14},{9,15},{10,... | collective-permute-start | bytes 393224 | tf_op jit(solution)/shard_map/ppermute | solution.py:377
  68.1 21.0 %collective-permute-start.6 = (f32[128,1024]{1,0:T(8,128)}, f32[128,1024]{1,0:T(8,128)S(1)}, u32[]{:S(2)}, u32[]{:S(2)}) collective-permute-start(f32[128,1024]{1,0:T(8,128)} %copy-done.20), channel_id=1, source_target_pairs={{0,1},{1,0},{2,3},{3,2},{4,5},{5,4},{6,7},{7,6},{8,9},{9,8},{10,11... | collective-permute-start | bytes 1572872 | tf_op jit(solution)/shard_map/ppermute | solution.py:360
  68.1 21.9 %collective-permute-start.10 = (f32[128,1024]{1,0:T(8,128)}, f32[128,1024]{1,0:T(8,128)S(1)}, u32[]{:S(2)}, u32[]{:S(2)}) collective-permute-start(f32[128,1024]{1,0:T(8,128)} %copy-done.22), channel_id=1, source_target_pairs={{0,1},{1,0},{2,3},{3,2},{4,5},{5,4},{6,7},{7,6},{8,9},{9,8},{10,11... | collective-permute-start | bytes 1572872 | tf_op jit(solution)/shard_map/ppermute | solution.py:394
  70.3 20.6 %collective-permute-start.9 = (f32[128,1024]{1,0:T(8,128)}, f32[128,1024]{1,0:T(8,128)S(1)}, u32[]{:S(2)}, u32[]{:S(2)}) collective-permute-start(f32[128,1024]{1,0:T(8,128)} %copy-done.21), channel_id=1, source_target_pairs={{0,1},{1,0},{2,3},{3,2},{4,5},{5,4},{6,7},{7,6},{8,9},{9,8},{10,11... | collective-permute-start | bytes 1572872 | tf_op jit(solution)/shard_map/ppermute | solution.py:393
  73.5 4.7 %collective-permute-start.14 = (f32[64,128]{1,0:T(8,128)S(1)}, f32[64,128]{1,0:T(8,128)S(1)}, u32[]{:S(2)}, u32[]{:S(2)}) collective-permute-start(f32[64,128]{1,0:T(8,128)S(1)} %get-tuple-element.66), channel_id=1, source_target_pairs={{0,0},{1,16},{2,2},{3,18},{4,4},{5,20},{6,6},{7,22},{8,1},{9,17},{... | collective-permute-start | bytes 98312 | tf_op jit(solution)/shard_map/ppermute | solution.py:390
  74.2 6.7 %collective-permute-start.15 = (f32[64,128]{1,0:T(8,128)S(1)}, f32[64,128]{1,0:T(8,128)S(1)}, u32[]{:S(2)}, u32[]{:S(2)}) collective-permute-start(f32[64,128]{1,0:T(8,128)S(1)} %get-tuple-element.63), channel_id=1, source_target_pairs={{0,1},{1,17},{2,3},{3,19},{4,5},{5,21},{6,7},{7,23},{8,0},{9,16},{... | collective-permute-start | bytes 98312 | tf_op jit(solution)/shard_map/ppermute | solution.py:390
  78.2 5.9 %collective-permute-start.16 = (f32[64,128]{1,0:T(8,128)S(1)}, f32[64,128]{1,0:T(8,128)S(1)}, u32[]{:S(2)}, u32[]{:S(2)}) collective-permute-start(f32[64,128]{1,0:T(8,128)S(1)} %get-tuple-element.65), channel_id=1, source_target_pairs={{0,8},{1,24},{2,10},{3,26},{4,12},{5,28},{6,14},{7,30},{8,9},{9,25... | collective-permute-start | bytes 98312 | tf_op jit(solution)/shard_map/ppermute | solution.py:390
  80.9 7.6 %collective-permute-start.17 = (f32[64,128]{1,0:T(8,128)S(1)}, f32[64,128]{1,0:T(8,128)S(1)}, u32[]{:S(2)}, u32[]{:S(2)}) collective-permute-start(f32[64,128]{1,0:T(8,128)S(1)} %get-tuple-element.64), channel_id=1, source_target_pairs={{0,9},{1,25},{2,11},{3,27},{4,13},{5,29},{6,15},{7,31},{8,8},{9,24... | collective-permute-start | bytes 98312 | tf_op jit(solution)/shard_map/ppermute | solution.py:390
  (17 other events, 31.2 us)

commit v2 on v1

v2 whole, which is shorter than its diff:
```python
import functools
import math

import jax
import jax.numpy as jnp
from jax import lax
from jax.experimental import pallas as pl
from jax.experimental.pallas import tpu as pltpu
from jax.sharding import PartitionSpec as P

F32 = jnp.float32
BF16 = jnp.bfloat16
SOME = 2
LIMIT = 8 << 20
CAST_LIMIT = 8 << 20
VM = pl.BlockSpec(memory_space=pltpu.VMEM)
SM = pl.BlockSpec(memory_space=pltpu.SMEM)
NN = (((1,), (0,)), ((), ()))
NT = (((1,), (1,)), ((), ()))
TN = (((0,), (0,)), ((), ()))


def split(x):
    hi = x.astype(BF16)
    return hi, (x - hi.astype(F32)).astype(BF16)


def dot(a, b, dims):
    return lax.dot_general(a, b, dims, preferred_element_type=F32)


def cat(parts, axis):
    return jnp.concatenate(parts, axis=axis)


def dot_wide(a, b, dims):
    ka, kb = dims[0][0][0], dims[0][1][0]
    hi, lo = split(a)
    return dot(cat([hi, lo], ka), cat([b, b], kb), dims)


def dot_full(a, b, dims):
    ka, kb = dims[0][0][0], dims[0][1][0]
    ah, al = split(a)
    bh, bl = split(b)
    return dot(cat([ah, al, ah], ka), cat([bh, bh, bl], kb), dims)


def softplus(x):
    z = jnp.exp(-jnp.abs(x))
    small = z * (1.0 - z * (0.5 - z * (1.0 / 3.0 - z * 0.25)))
    return jnp.maximum(x, 0.0) + jnp.where(z < 0.03, small, jnp.log(1.0 + z))


def heads_loop(first, last, load, work, store, some=SOME):
    some = math.gcd(some, last - first)

    def body(p, _):
        hs = [first + p * some + u for u in range(some)]
        outs = [work(*x) for x in [load(h) for h in hs]]
        for h, out in zip(hs, outs):
            store(h, *out)
        return 0

    lax.fori_loop(0, (last - first) // some, body, 0)


class Docs:
    def __init__(self, lengths_ref, ndoc, rows):
        self.rows = rows
        self.first = (lax.axis_index("ctx") // 2) * rows
        self.starts = [jnp.int32(0)]
        for d in range(ndoc):
            self.starts.append(self.starts[-1] + lengths_ref[0, d])

    def start_of(self, pos):
        out = jnp.zeros_like(pos)
        for s in self.starts[1:]:
            out = jnp.where(pos >= s, s, out)
        return out

    def along(self, axis, shape):
        return self.first + lax.broadcasted_iota(jnp.int32, shape, axis)

    def keep_t(self):
        shape = (self.rows, self.rows)
        s, t = self.along(0, shape), self.along(1, shape)
        begin = self.start_of(self.along(1, (8, self.rows)))[:1]
        return ((s <= t) & (s >= begin)).astype(F32)

    def inside_row(self):
        return (self.start_of(self.along(1, (8, self.rows))) < self.first).astype(F32)[:1]

    def head_row(self):
        begin = self.start_of(self.along(1, (8, self.rows)))
        return (begin <= self.first).astype(F32)[:1]

    def tail_row(self):
        last = self.start_of(self.first + self.rows - 1 + jnp.int32(0))
        return (self.along(1, (8, self.rows)) >= last).astype(F32)[:1]

    def later_col(self, width):
        after = self.start_of(self.first + self.rows + jnp.int32(0))
        return (self.along(0, (self.rows, width)) >= after).astype(F32)


def my_core():
    return lax.rem(lax.axis_index("ctx"), 2)


def place(ref, h, width):
    return ref[:, pl.ds(pl.multiple_of(h * width, width), width)]


def token_pair(own_ref, got_ref, h, width):
    core = my_core()
    own = place(own_ref, h, width).astype(F32)
    got = place(got_ref, h, width)
    first = jnp.where(core == 0, own, got)
    second = jnp.where(core == 0, got, own)
    return cat([first, second], 0).astype(BF16)


def cast_kernel(k_ref, v_ref, q_ref, g_ref, w_ref, ko_ref, vo_ref, qo_ref, go_ref,
                ks_ref, vs_ref, qs_ref, gs_ref, wo_ref, bufs, sems):
    core = my_core()
    refs = [k_ref, v_ref, q_ref, g_ref]
    owns = [ko_ref, vo_ref, qo_ref, go_ref]
    sends = [ks_ref, vs_ref, qs_ref, gs_ref]
    half = ko_ref.shape[1]
    nh = wo_ref.shape[0]
    mine = pl.ds(pl.multiple_of(core * half, half), half)
    other = pl.ds(pl.multiple_of((1 - core) * half, half), half)
    out = [pltpu.make_async_copy(r.at[:, other], bufs.at[i], sems.at[i]) for i, r in enumerate(refs)]
    keep = [pltpu.make_async_copy(r.at[:, mine], o, sems.at[4 + i])
            for i, (r, o) in enumerate(zip(refs, owns))]
    keep.append(pltpu.make_async_copy(w_ref.at[pl.ds(core * nh, nh)], wo_ref, sems.at[8]))
    for c in out + keep:
        c.start()
    for i, c in enumerate(out):
        c.wait()
        sends[i][...] = bufs[i].astype(F32)
    for c in keep:
        c.wait()


def mask_kernel(ndoc, len_ref, keep_ref, line_ref, later_ref):
    docs = Docs(len_ref, ndoc, keep_ref.shape[0])
    keep_ref[...] = docs.keep_t()
    line_ref[...] = cat([docs.inside_row(), docs.head_row(), docs.tail_row()] + [docs.tail_row()] * 5, 0)
    later_ref[...] = docs.later_col(later_ref.shape[1])


def key_kernel(nh, k_ref, v_ref, kg_ref, vg_ref, w_ref, line_ref,
               fk_ref, fkt_ref, k2_ref, v2_ref, s1_ref, s2_ref):
    _, width = fk_ref.shape[1:]
    few = nh - s2_ref.shape[0]
    tail = line_ref[2:3]

    def load(h):
        return (token_pair(k_ref, kg_ref, h, width), token_pair(v_ref, vg_ref, h, width),
                w_ref[h])

    def work(k, v, w):
        fk = softplus(dot(k, w, NN))
        fkt = fk.T
        masked = fkt * tail
        norm = jnp.broadcast_to(jnp.sum(masked, axis=1, keepdims=True), (width, 128)).T[:1]
        return fk, fkt, k, v, dot_wide(masked, v, NN), norm

    def store(h, fk, fkt, k, v, s, n):
        fk_ref[h] = fk
        fkt_ref[h] = fkt
        k2_ref[h] = k
        v2_ref[h] = v
        s1_ref[pl.ds(few * width + h, 1)] = n
        return s

    def store1(h, *out):
        s1_ref[pl.ds(pl.multiple_of(h * width, width), width)] = store(h, *out)

    def store2(h, *out):
        s2_ref[h - few] = store(h, *out)

    heads_loop(0, few, load, work, store1)
    heads_loop(few, nh, load, work, store2)


def query_kernel(nh, q_ref, g_ref, qg_ref, gg_ref, w_ref, fk_ref, keep_ref,
                 fqt_ref, pqt_ref, q2_ref, g2_ref, at_ref, dl_ref):
    _, width = fk_ref.shape[1:]

    def load(h):
        return (token_pair(q_ref, qg_ref, h, width), token_pair(g_ref, gg_ref, h, width),
                w_ref[h], fk_ref[h])

    def work(q, g, w, fk):
        pre = dot(q, w, NN).T
        fqt = softplus(pre)
        at = dot_full(fk, fqt, NN) * keep_ref[...]
        return q, g, pre, fqt, at, jnp.sum(at, axis=0, keepdims=True)

    def store(h, q, g, pre, fqt, at, dl):
        q2_ref[h] = q
        g2_ref[h] = g
        pqt_ref[h] = pre
        fqt_ref[h] = fqt
        at_ref[h] = at
        dl_ref[h] = dl

    heads_loop(0, nh, load, work, store)


def rstate_kernel(nh, few, line_ref, fqt_ref, g2_ref, dl_ref, s1_ref, inv_ref, r_ref):
    width = fqt_ref.shape[1]
    inside, head = line_ref[:1], line_ref[1:2]

    def load(h):
        return fqt_ref[h], g2_ref[h], dl_ref[h], s1_ref[pl.ds(few * width + h, 1)]

    def work(fqt, g, dl, n):
        norm = jnp.broadcast_to(n, (8, n.shape[1]))
        denom = dl + inside * dot_full(norm, fqt, NN)[:1]
        inv = 1.0 / denom
        return inv, dot_wide(fqt * (inv * head), g, NN)

    def store(h, inv, r):
        inv_ref[h] = inv
        r_ref[h] = r

    heads_loop(0, nh, load, work, store, 2 * SOME)


def fill_kernel(nh, at_ref, inv_ref, g2_ref, v2_ref, k2_ref, w_ref, fk_ref, pqt_ref, fqt_ref,
                mt_ref, cl_ref, gv_ref, sk_ref, sqt_ref):
    def load(h):
        return (at_ref[h], inv_ref[h], g2_ref[h], v2_ref[h], k2_ref[h], w_ref[h],
                fk_ref[h], pqt_ref[h], fqt_ref[h])

    def work(at, inv, g, v, k, w, fk, pqt, fqt):
        mt = dot(v, g, NT)
        cl = jnp.sum(at * mt, axis=0, keepdims=True)
        gv = dot_wide(at * inv, g, NN)
        return mt, cl, gv, jnp.exp(dot(k, w, NN) - fk), jnp.exp(pqt - fqt)

    def store(h, mt, cl, gv, sk, sqt):
        mt_ref[h] = mt
        cl_ref[h] = cl
        gv_ref[h] = gv
        sk_ref[h] = sk
        sqt_ref[h] = sqt

    heads_loop(0, nh, load, work, store)


def out_pair(x, own_ref, send_ref, h, width):
    core = my_core()
    half = x.shape[0] // 2
    own = jnp.where(core == 0, x[:half], x[half:])
    other = jnp.where(core == 0, x[half:], x[:half])
    at = pl.ds(pl.multiple_of(h * width, width), width)
    own_ref[:, at] = own.astype(BF16)
    send_ref[:, at] = other


def shift_kernel(nh, line_ref, s1_ref, s2_ref, cl_ref, inv_ref, g2_ref, fqt_ref,
                 rn_ref, ut_ref, c_ref):
    rows = fqt_ref.shape[2]
    inside, head = line_ref[:1], line_ref[1:2]

    width = fqt_ref.shape[1]
    few = nh - s2_ref.shape[0]

    def load1(h):
        s = s1_ref[pl.ds(pl.multiple_of(h * width, width), width)]
        return s, cl_ref[h], inv_ref[h], g2_ref[h], fqt_ref[h]

    def load2(h):
        return s2_ref[h - few], cl_ref[h], inv_ref[h], g2_ref[h], fqt_ref[h]

    def work(s, cl, inv, g, fqt):
        ut = dot_wide(s, g, NT)
        c = (cl + inside * jnp.sum(fqt * ut, axis=0, keepdims=True)) * inv
        rn = dot_full(jnp.broadcast_to(-c * inv * head, (8, rows)), fqt, NT)[:1]
        return rn, ut, c

    def store(h, rn, ut, c):
        rn_ref[h] = rn
        ut_ref[h] = ut
        c_ref[h] = c

    heads_loop(0, few, load1, work, store)
    heads_loop(few, nh, load2, work, store)


def forward_kernel(nh, few, line_ref, keep_ref, ut_ref, c_ref, s1_ref, mt_ref, inv_ref, q2_ref,
                   fqt_ref, sqt_ref, fkt_ref, w_ref,
                   gq_ref, gqs_ref, qt_ref, gfk_ref):
    rows, width = gfk_ref.shape[1:]
    inside = line_ref[:1]

    def load(h):
        return (ut_ref[h], c_ref[h], s1_ref[pl.ds(few * width + h, 1)], mt_ref[h], inv_ref[h], q2_ref[h],
                fqt_ref[h], sqt_ref[h], fkt_ref[h], w_ref[h])

    def work(ut, c, n, mt, inv, q, fqt, sqt, fkt, w):
        pt = (mt - c) * inv * keep_ref[...]
        gfk = dot_full(pt, fqt, NT)
        norm = jnp.broadcast_to(n, (width, width)).T
        carried = (ut - cat([norm] * (rows // width), 1) * c) * inv
        gpq = (dot_full(fkt, pt, NN) + inside * carried) * sqt
        hi, lo = split(gpq)
        gq = dot(cat([w, w], 1), cat([hi, lo], 0), NN).T
        qt = dot(cat([hi, lo], 1), cat([q, q], 0), NN).T
        return gq, qt, gfk

    def store(h, gq, qt, gfk):
        out_pair(gq, gq_ref, gqs_ref, h, width)
        qt_ref[h] = qt
        gfk_ref[h] = gfk

    heads_loop(0, nh, load, work, store)


def backward_kernel(nh, factor, later_ref, r_ref, rn_ref, gfk_ref, gv0_ref, sk_ref, fk_ref,
                    k2_ref, v2_ref, qt_ref, w_ref,
                    gk_ref, gks_ref, gv_ref, gvs_ref, *more_refs):
    *plane_refs, wt_ref = more_refs
    _, width = fk_ref.shape[1:]
    low, both, _ = plane_refs[0].shape
    chips = len(plane_refs)
    pieces = width // both

    def load(h):
        return (r_ref[h], rn_ref[h], gfk_ref[h], gv0_ref[h], sk_ref[h], fk_ref[h],
                k2_ref[h], v2_ref[h], qt_ref[h], w_ref[h])

    def work(r, rn, gfk, gv0, sk, fk, k, v, qt, w):
        rh, rl = split(r)
        carried = dot(cat([v, v], 1), cat([rh, rl], 1), NT) + rn
        gpk = (gfk + later_ref[...] * carried) * sk
        hi, lo = split(gpk)
        wt = (dot(cat([k, k], 0), cat([hi, lo], 0), TN) + qt) * factor
        gk = dot(cat([hi, lo], 1), cat([w, w], 1), NT)
        fh, fl = split(fk)
        gv = gv0 + later_ref[...] * dot(cat([fh, fl, fh], 1), cat([rh, rh, rl], 0), NN)
        return wt, gk, gv

    def store(h, wt, gk, gv):
        for p in range(pieces):
            wt_ref[h * pieces + p] = wt[p * both : (p + 1) * both]
        out_pair(gk, gk_ref, gks_ref, h, width)
        out_pair(gv, gv_ref, gvs_ref, h, width)

    heads_loop(0, nh, load, work, store)
    chip = lax.axis_index("ctx") // 2
    for j, ref in enumerate(plane_refs):
        for z in range(low):
            ref[z] = wt_ref[z * chips + (chip ^ j)]


def fold_kernel(bit, parts, *refs):
    ins, outs = refs[:parts], refs[parts:]
    here = bit and bit()
    for i in range(outs[0].shape[0]):
        if bit is None:
            outs[0][i] = functools.reduce(jnp.add, [r[i] for r in ins])
        else:
            a = functools.reduce(jnp.add, [r[2 * i] for r in ins])
            b = functools.reduce(jnp.add, [r[2 * i + 1] for r in ins])
            outs[0][i] = jnp.where(here == 0, a, b)
            outs[1][i] = jnp.where(here == 0, b, a)


def pick_kernel(bit, own_ref, got_ref, keep_ref, send_ref):
    here = bit()
    own, got = own_ref[...], got_ref[...]
    keep_ref[...] = jnp.where(here == 0, own, got)
    send_ref[...] = jnp.where(here == 0, got, own)


def join_kernel(own_ref, got_ref, out_ref):
    core = my_core()
    half = own_ref.shape[1]
    out_ref[:, pl.ds(pl.multiple_of(core * half, half), half)] = own_ref[...]
    out_ref[:, pl.ds(pl.multiple_of((1 - core) * half, half), half)] = got_ref[...].astype(BF16)


def dp_bit(step):
    return (lax.axis_index("dp") // step) % 2


def call(kernel, outs, smem=0, hbm=0, scratch=(), limit=LIMIT):
    def run(*args):
        rest = len(args) - smem - hbm
        return pl.pallas_call(
            kernel,
            out_shape=[jax.ShapeDtypeStruct(s, d) for s, d in outs],
            in_specs=[SM] * smem + [pl.BlockSpec(memory_space=pltpu.HBM)] * hbm + [VM] * rest,
            out_specs=[VM] * len(outs),
            scratch_shapes=list(scratch),
            compiler_params=pltpu.CompilerParams(vmem_limit_bytes=limit),
        )(*args)

    return run


def shards(queries, keys, values, out_grad, feature_weight, doc_lengths):
    ctx = lax.axis_size("ctx")
    dp = lax.axis_size("dp")
    tok = queries.shape[1]
    heads, width, _ = feature_weight.shape
    ndoc = doc_lengths.shape[1]
    chips = ctx // 2
    nh = heads // 2
    rows = 2 * tok
    longest = ctx * tok // 4
    hops = -(-longest // rows)
    factor = 1.0 / math.sqrt(dp * ctx * tok)

    swap = [(i, i ^ 1) for i in range(ctx)]
    ahead = [(i, i + 2) for i in range(ctx - 2)]
    back = [(i + 2, i) for i in range(ctx - 2)]

    q, k, v, g = queries[0], keys[0], values[0], out_grad[0]
    w = feature_weight
    half = (tok, nh * width)

    def swapped(*arrays):
        return [lax.ppermute(x, "ctx", swap) for x in arrays]

    wide = (nh, rows, width)
    tall = (nh, width, rows)
    square = (nh, rows, rows)
    state = (nh, width, width)
    norm = (nh, 1, width)
    line = (nh, 1, rows)

    few = max(1, nh // 4)

    ko, vo, qo, go, ks, vs, qs, gs, w = call(
        cast_kernel, [(half, BF16)] * 4 + [(half, F32)] * 4 + [((nh, width, width), BF16)],
        0, 5, [pltpu.VMEM((4,) + half, BF16), pltpu.SemaphoreType.DMA((9,))], CAST_LIMIT,
    )(*[pltpu.with_memory_space_constraint(x, pltpu.HBM) for x in (k, v, q, g, w)])
    kg, vg = swapped(ks, vs)
    qg, gg = swapped(qs, gs)
    keep, lines, later = call(
        functools.partial(mask_kernel, ndoc),
        [((rows, rows), F32), ((8, rows), F32), ((rows, width), F32)],
        1,
    )(doc_lengths)

    if hops > 1:
        ends = jnp.cumsum(doc_lengths[0])
        begins = jnp.concatenate([jnp.zeros((1,), jnp.int32), ends])

        chip = lax.axis_index("ctx") // 2

        def start_of(p):
            return jnp.max(jnp.where(begins <= p, begins, 0))

    def carry(x, forward):
        total = moved = lax.ppermute(x, "ctx", ahead if forward else back)
        for h in range(1, hops):
            moved = lax.ppermute(moved, "ctx", ahead if forward else back)
            if forward:
                gate = start_of(chip * rows) < (chip - h) * rows
            else:
                gate = start_of((chip + 1 + h) * rows) < (chip + 1) * rows
            total = total + jnp.where(gate, moved, 0.0)
        return total

    fk, fkt, k2, v2, s1, s2 = call(
        functools.partial(key_kernel, nh),
        [(wide, F32), (tall, F32), (wide, BF16), (wide, BF16),
         ((few * width + -(-nh // 8) * 8, width), F32), ((nh - few, width, width), F32)],
    )(ko, vo, kg, vg, w, lines)
    s1 = carry(s1, True)
    s2 = carry(s2, True)
    fqt, pqt, q2, g2, at, dl = call(
        functools.partial(query_kernel, nh),
        [(tall, F32), (tall, F32), (wide, BF16), (wide, BF16), (square, F32), (line, F32)],
    )(qo, go, qg, gg, w, fk, keep)
    inv, r_loc = call(
        functools.partial(rstate_kernel, nh, few), [(line, F32), (state, F32)]
    )(lines, fqt, g2, dl, s1)
    r_in = carry(r_loc, False)
    mt, cl, gv0, sk, sqt = call(
        functools.partial(fill_kernel, nh),
        [(square, F32), (line, F32), (wide, F32), (wide, F32), (tall, F32)],
    )(at, inv, g2, v2, k2, w, fk, pqt, fqt)
    rn, ut, c = call(
        functools.partial(shift_kernel, nh), [(norm, F32), (tall, F32), (line, F32)]
    )(lines, s1, s2, cl, inv, g2, fqt)
    rn_in = carry(rn, False)
    gq, gqs, qt, gfk = call(
        functools.partial(forward_kernel, nh, few),
        [(half, BF16), (half, F32), (state, F32), (wide, F32)],
    )(lines, keep, ut, c, s1, mt, inv, q2, fqt, sqt, fkt, w)

    each = heads * width // (dp * ctx)
    low = dp // 2
    gk, gks, gv, gvs, *planes = call(
        functools.partial(backward_kernel, nh, factor),
        [(half, BF16), (half, F32), (half, BF16), (half, F32)] + [((low, 2 * each, width), F32)] * chips,
        scratch=[pltpu.VMEM((low * chips, 2 * each, width), F32)],
    )(later, r_in, rn_in, gfk, gv0, sk, fk, k2, v2, qt, w)

    def join(own, got):
        return call(join_kernel, [((tok, heads * width), BF16)])(own, got)[0][None]

    moved = []
    for j in range(1, chips):
        perm = [(i, ((i // 2) ^ j) * 2 + i % 2) for i in range(ctx)]
        moved.append(lax.ppermute(planes[j], "ctx", perm))
    gqs, gks, gvs = lax.optimization_barrier((gqs, gks, gvs, planes[0]))[:3]
    gqg, gkg, gvg = swapped(gqs, gks, gvs)
    out_q, out_k, out_v = join(gq, gqg), join(gk, gkg), join(gv, gvg)

    def folded(parts, size, bit):
        return call(
            functools.partial(fold_kernel, bit, len(parts)),
            [(size, F32)] * (1 if bit is None else 2),
        )(*parts)

    parts = [planes[0]] + moved
    left, step = low, 1
    while left > 1:
        left //= 2
        kept, sent = folded(parts, (left, 2 * each, width), functools.partial(dp_bit, step))
        if step == 1:
            sent, out_q, out_k, out_v = lax.optimization_barrier((sent, out_q, out_k, out_v))
        parts = [kept, lax.ppermute(sent, "dp", [(i, i ^ step) for i in range(dp)])]
        step *= 2
    parts = [x.reshape(2, each, width) for x in parts]
    kept, sent = folded(parts, (1, each, width), my_core)
    (got,) = swapped(sent)
    kept, sent = call(
        functools.partial(pick_kernel, lambda: dp_bit(step) ^ my_core()),
        [((1, each, width), F32)] * 2,
    )(kept, got)
    parts = [kept, lax.ppermute(sent, "dp", [(i, i ^ step) for i in range(dp)])]
    (grad_weight,) = folded(parts, (1, each, width), None)
    return (out_q, out_k, out_v, grad_weight[0])


def solution(mesh):
    placed = (
        P("dp", "ctx", None),
        P("dp", "ctx", None),
        P("dp", "ctx", None),
        P("dp", "ctx", None),
        P(),
        P("dp", None),
    )
    return jax.shard_map(
        shards,
        mesh=mesh,
        in_specs=placed,
        out_specs=(
            P("dp", "ctx", None),
            P("dp", "ctx", None),
            P("dp", "ctx", None),
            P(("dp", "ctx"), None),
        ),
        check_vma=False,
    )
```

time: 92.2 us -> 79.1 us (0.86)
  local copies, waits for them, and re-layouts: 10.9 us -> 0.01 us
  waiting for transfers between devices: 17.6 us -> 26.5 us
  Pallas kernels: 30.1 us -> 23.1 us
  other arithmetic: 4.79 us -> 0 us
  starting transfers between devices: 27.4 us -> 28.6 us
    unnamed x46 -> x2, local copies, waits for them, and re-layouts: 10.9 us -> 0.01 us
    pallas_call x9 -> x16, Pallas kernels: 30.1 us -> 23.1 us  [run(): pl.pallas_call(kernel, out_shape=[jax.ShapeDtypeStruct(s, d) for s, d in...]
    ppermute x4, waiting for transfers between devices: 8.51 us -> 14.3 us  [carry(): total = moved = lax.ppermute(x, 'ctx', ahead if forward else back)]
    convert_element_type x4 -> x0, other arithmetic: 3.23 us -> none  [other_half(): return lax.ppermute(part.astype(F32), 'ctx', swap)]
    ppermute x14 -> x13, waiting for transfers between devices: 9.08 us -> 12.1 us  [the longest x2 5.26 us: shards(): parts = [kept, lax.ppermute(sent, 'dp', [(i, i ^ step) for i in range(dp)])]]
    ppermute x4, starting transfers between devices: 10.7 us -> 12.4 us  [carry(): total = moved = lax.ppermute(x, 'ctx', ahead if forward else back)]
    add x2 -> x0, other arithmetic: 1.57 us -> none  [the longest x1 0.94 us: shards(): total = total + part]
    ppermute x14 -> x13, starting transfers between devices: 16.7 us -> 16.2 us  [the longest x3 10.1 us: shards(): moved.append(lax.ppermute(planes[j], 'ctx', perm))]
  transfers between devices with their start and end apart: 18 -> 17, of which waited for: 8 -> 10; matrix products, arithmetic and copies ran while one was open for 4% -> 0% of each run, Pallas kernels for 27% -> 20%
where the time goes in v2:
time: 79.1 us; the launch traced here: 78.9 us
  starting transfers between devices  28.6 us (36%)
  waiting for transfers between devices  26.5 us (34%)
  Pallas kernels  23.1 us (29%)
    pallas_call x16, Pallas kernels, run(): pl.pallas_call(kernel, out_shape=[jax.ShapeDtypeStruct(s, d) for s, d in...  23.1 us
    ppermute x4, waiting for transfers between devices, carry(): total = moved = lax.ppermute(x, 'ctx', ahead if forward else back)  14.3 us
    ppermute x4, starting transfers between devices, carry(): total = moved = lax.ppermute(x, 'ctx', ahead if forward else back)  12.4 us
    ppermute x3, starting transfers between devices, shards(): moved.append(lax.ppermute(planes[j], 'ctx', perm))  10.1 us
    ppermute x2, waiting for transfers between devices, shards(): parts = [kept, lax.ppermute(sent, 'dp', [(i, i ^ step) for i in range(dp)])]  5.26 us
    ppermute x3, waiting for transfers between devices, shards(): moved.append(lax.ppermute(planes[j], 'ctx', perm))  4.57 us
    ppermute x2, starting transfers between devices, shards(): parts = [kept, lax.ppermute(sent, 'dp', [(i, i ^ step) for i in range(dp)])]  4.23 us
    ppermute x8, waiting for transfers between devices, swapped(): return [lax.ppermute(x, 'ctx', swap) for x in arrays]  2.28 us
  transfers between devices with their start and end apart: 17, of which 10 were waited for; matrix products, arithmetic and copies ran while one was open for 0% of the time, Pallas kernels for 20%

profile of v2, /device:TPU:0, one launch (start us, length us, event | category | flops | bytes accessed | tf_op | source)
XLA Modules:
  0.0 78.9 jit_solution(3717315563142906142)
XLA Ops:
  0.6 1.7 %shard_map.94 = (bf16[128,1024]{1,0:T(8,128)(2,1)S(1)}, bf16[128,1024]{1,0:T(8,128)(2,1)S(1)}, bf16[128,1024]{1,0:T(8,128)(2,1)S(1)}, bf16[128,1024]{1,0:T(8,128...) custom-call(bf16[128,2048]{1,0:T(8,128)(2,1)} %bitcast.12, ...), custom_call_target="tpu_custom_call" | custom-call | tf_op jit(solution)/shard_map/pallas_call | solution.py:396
  5.2 3.0 %shard_map.95 = (f32[8,256,128]{2,1,0:T(8,128)S(1)}, f32[8,128,256]{2,1,0:T(8,128)S(1)}, bf16[8,256,128]{2,1,0:T(8,128)(2,1)S(1)}, bf16[8,256,128]{2,1,0:T(8,128...) custom-call(bf16[128,1024]{1,0:T(8,128)(2,1)S(1)} %get-tuple-element.70.k_ref, ...), custom_call_target="tpu_custom_call" | custom-call | tf_op jit(solution)/shard_map/pallas_call | solution.py:396
  8.2 4.8 %collective-permute-start.4 = (f32[264,128]{1,0:T(8,128)S(1)}, f32[264,128]{1,0:T(8,128)S(1)}, u32[]{:S(2)}, u32[]{:S(2)}) collective-permute-start(f32[264,128]{1,0:T(8,128)S(1)} %get-tuple-element.79), channel_id=1, source_target_pairs={{0,2},{1,3},{2,4},{3,5},{4,6},{5,7},{8,10},{9,11},{10,12},{11,13},... | collective-permute-start | bytes 405512 | tf_op jit(solution)/shard_map/ppermute | solution.py:463
  13.0 3.0 %shard_map.96 = (f32[8,128,256]{2,1,0:T(8,128)S(1)}, f32[8,128,256]{2,1,0:T(8,128)S(1)}, bf16[8,256,128]{2,1,0:T(8,128)(2,1)S(1)}, bf16[8,256,128]{2,1,0:T(8,128...) custom-call(bf16[128,1024]{1,0:T(8,128)(2,1)S(1)} %get-tuple-element.65.q_ref, ...), custom_call_target="tpu_custom_call" | custom-call | tf_op jit(solution)/shard_map/pallas_call | solution.py:396
  16.1 1.6 %shard_map.97 = (f32[8,1,256]{2,1,0:T(1,128)S(1)}, f32[8,128,128]{2,1,0:T(8,128)S(1)}) custom-call(f32[8,256]{1,0:T(8,128)S(1)} %get-tuple-element.64.line_ref, f32[8,128,256]{2,1,0:T(8,128)S(1)} %get-tuple-element.76.fqt_ref, bf16[8,256,128]{2,1,0:T(8,128)(2,1)S(1)} %get-tuple-element.77.g2_ref, f32[8,1,256]{2,1,0:T(1,128)S(1)} %get-tuple-element.78.dl_ref, ...), custom_call_target="tpu_custom_call" | custom-call | tf_op jit(solution)/shard_map/pallas_call | solution.py:396
  17.6 1.3 %collective-permute-start.5 = (f32[8,128,128]{2,1,0:T(8,128)S(1)}, f32[8,128,128]{2,1,0:T(8,128)S(1)}, u32[]{:S(2)}, u32[]{:S(2)}) collective-permute-start(f32[8,128,128]{2,1,0:T(8,128)S(1)} %get-tuple-element.80), channel_id=1, source_target_pairs={{2,0},{3,1},{4,2},{5,3},{6,4},{7,5},{10,8},{11,9},{12,10},{13,11},... | collective-permute-start | bytes 1572872 | tf_op jit(solution)/shard_map/ppermute | solution.py:463
  18.9 5.0 %collective-permute-start.6 = (f32[6,128,128]{2,1,0:T(8,128)S(1)}, f32[6,128,128]{2,1,0:T(8,128)S(1)}, u32[]{:S(2)}, u32[]{:S(2)}) collective-permute-start(f32[6,128,128]{2,1,0:T(8,128)S(1)} %get-tuple-element.81), channel_id=1, source_target_pairs={{0,2},{1,3},{2,4},{3,5},{4,6},{5,7},{8,10},{9,11},{10,12},{11,13},... | collective-permute-start | bytes 1179656 | tf_op jit(solution)/shard_map/ppermute | solution.py:463
  24.0 1.6 %shard_map.98 = (f32[8,256,256]{2,1,0:T(8,128)S(1)}, f32[8,1,256]{2,1,0:T(1,128)S(1)}, f32[8,256,128]{2,1,0:T(8,128)S(1)}, f32[8,256,128]{2,1,0:T(8,128)S(1)}, f32[8,128,256]{2,1,0:T(8,128)S(1)}) custom-call(f32[8,256,256]{2,1,0:T(8,128)S(1)} %get-tuple-element.82.at_ref, f32[8,1,256]{2,1,0:T(1,128)S(1)} %get-tuple-element.83.inv_ref, ...), custom_call_target="tpu_custom_call" | custom-call | tf_op jit(solution)/shard_map/pallas_call | solution.py:396
  25.6 6.2 %collective-permute-done.6.s2_ref = f32[6,128,128]{2,1,0:T(8,128)S(1)} collective-permute-done((f32[6,128,128]{2,1,0:T(8,128)S(1)}, f32[6,128,128]{2,1,0:T(8,128)S(1)}, u32[]{:S(2)}, u32[]{:S(2)}) %collective-permute-start.6) | collective-permute-done | bytes 393248 | tf_op jit(solution)/shard_map/ppermute | solution.py:463
  31.8 1.9 %shard_map.99 = (f32[8,1,128]{2,1,0:T(1,128)S(1)}, f32[8,128,256]{2,1,0:T(8,128)S(1)}, f32[8,1,256]{2,1,0:T(1,128)S(1)}) custom-call(f32[8,256]{1,0:T(8,128)S(1)} %get-tuple-element.64.line_ref, f32[264,128]{1,0:T(8,128)S(1)} %collective-permute-done.4.s1_ref, f32[6,128,128]{2,1,0:T(8,128)S(1)} %collective-permute-done.6.s2_ref, ...), custom_call_target="tpu_custom_call" | custom-call | tf_op jit(solution)/shard_map/pallas_call | solution.py:396
  33.7 1.3 %collective-permute-start.7 = (f32[8,1,128]{2,1,0:T(1,128)S(1)}, f32[8,1,128]{2,1,0:T(1,128)S(1)}, u32[]{:S(2)}, u32[]{:S(2)}) collective-permute-start(f32[8,1,128]{2,1,0:T(1,128)S(1)} %get-tuple-element.88), channel_id=1, source_target_pairs={{2,0},{3,1},{4,2},{5,3},{6,4},{7,5},{10,8},{11,9},{12,10},{13,11},... | collective-permute-start | bytes 12296 | tf_op jit(solution)/shard_map/ppermute | solution.py:463
  35.0 3.7 %shard_map.100 = (bf16[128,1024]{1,0:T(8,128)(2,1)S(1)}, f32[128,1024]{1,0:T(8,128)S(1)}, f32[8,128,128]{2,1,0:T(8,128)S(1)}, f32[8,256,128]{2,1,0:T(8,128)S(1)}) custom-call(f32[8,256]{1,0:T(8,128)S(1)} %get-tuple-element.64.line_ref, f32[256,256]{1,0:T(8,128)S(1)} %get-tuple-element.75.keep_ref, f32[8,128,256]{2,1,0:T(8,128)S(1)} %get-tuple-element.89.ut_ref, ...), custom_call_target="tpu_custom_call" | custom-call | tf_op jit(solution)/shard_map/pallas_call | solution.py:396
  38.7 8.1 %collective-permute-done.7.rn_ref = f32[8,1,128]{2,1,0:T(1,128)S(1)} collective-permute-done((f32[8,1,128]{2,1,0:T(1,128)S(1)}, f32[8,1,128]{2,1,0:T(1,128)S(1)}, u32[]{:S(2)}, u32[]{:S(2)}) %collective-permute-start.7) | collective-permute-done | bytes 4128 | tf_op jit(solution)/shard_map/ppermute | solution.py:463
  46.8 2.8 %shard_map.101 = (bf16[128,1024]{1,0:T(8,128)(2,1)S(1)}, f32[128,1024]{1,0:T(8,128)S(1)}, bf16[128,1024]{1,0:T(8,128)(2,1)S(1)}, f32[128,1024]{1,0:T(8,128)S(1)}...) custom-call(f32[256,128]{1,0:T(8,128)S(1)} %get-tuple-element.63.lat, ...), custom_call_target="tpu_custom_call" | custom-call | tf_op jit(solution)/shard_map/pallas_call | solution.py:396
  50.2 3.4 %collective-permute-start.8 = (f32[2,128,128]{2,1,0:T(8,128)S(1)}, f32[2,128,128]{2,1,0:T(8,128)S(1)}, u32[]{:S(2)}, u32[]{:S(2)}) collective-permute-start(f32[2,128,128]{2,1,0:T(8,128)S(1)} %get-tuple-element.100), channel_id=1, source_target_pairs={{0,2},{1,3},{2,0},{3,1},{4,6},{5,7},{6,4},{7,5},{8,10},{9,11},{10,... | collective-permute-start | bytes 393224 | tf_op jit(solution)/shard_map/ppermute | solution.py:515
  53.6 2.7 %collective-permute-start.9 = (f32[2,128,128]{2,1,0:T(8,128)S(1)}, f32[2,128,128]{2,1,0:T(8,128)S(1)}, u32[]{:S(2)}, u32[]{:S(2)}) collective-permute-start(f32[2,128,128]{2,1,0:T(8,128)S(1)} %get-tuple-element.101), channel_id=1, source_target_pairs={{0,4},{1,5},{2,6},{3,7},{4,0},{5,1},{6,2},{7,3},{8,12},{9,13},{10,... | collective-permute-start | bytes 393224 | tf_op jit(solution)/shard_map/ppermute | solution.py:515
  56.3 1.3 %collective-permute-done.8.refs_1_ = f32[2,128,128]{2,1,0:T(8,128)S(1)} collective-permute-done((f32[2,128,128]{2,1,0:T(8,128)S(1)}, f32[2,128,128]{2,1,0:T(8,128)S(1)}, u32[]{:S(2)}, u32[]{:S(2)}) %collective-permute-start.8) | collective-permute-done | bytes 131104 | tf_op jit(solution)/shard_map/ppermute | solution.py:515
  57.7 3.9 %collective-permute-start.10 = (f32[2,128,128]{2,1,0:T(8,128)S(1)}, f32[2,128,128]{2,1,0:T(8,128)S(1)}, u32[]{:S(2)}, u32[]{:S(2)}) collective-permute-start(f32[2,128,128]{2,1,0:T(8,128)S(1)} %get-tuple-element.102), channel_id=1, source_target_pairs={{0,6},{1,7},{2,4},{3,5},{4,2},{5,3},{6,0},{7,1},{8,14},{9,15},{10,... | collective-permute-start | bytes 393224 | tf_op jit(solution)/shard_map/ppermute | solution.py:515
  61.6 3.2 %collective-permute-done.10.refs_3_ = f32[2,128,128]{2,1,0:T(8,128)S(1)} collective-permute-done((f32[2,128,128]{2,1,0:T(8,128)S(1)}, f32[2,128,128]{2,1,0:T(8,128)S(1)}, u32[]{:S(2)}, u32[]{:S(2)}) %collective-permute-start.10) | collective-permute-done | bytes 131104 | tf_op jit(solution)/shard_map/ppermute | solution.py:515
  67.4 1.6 %collective-permute-start.14 = (f32[1,128,128]{2,1,0:T(8,128)S(1)}, f32[1,128,128]{2,1,0:T(8,128)S(1)}, u32[]{:S(2)}, u32[]{:S(2)}) collective-permute-start(f32[1,128,128]{2,1,0:T(8,128)S(1)} %get-tuple-element.117), channel_id=1, source_target_pairs={{0,8},{8,0},{16,24},{24,16},{1,9},{9,1},{17,25},{25,17},{2,10},{10... | collective-permute-start | bytes 196616 | tf_op jit(solution)/shard_map/ppermute | solution.py:533
  69.0 2.7 %collective-permute-done.14 = f32[1,128,128]{2,1,0:T(8,128)S(1)} collective-permute-done((f32[1,128,128]{2,1,0:T(8,128)S(1)}, f32[1,128,128]{2,1,0:T(8,128)S(1)}, u32[]{:S(2)}, u32[]{:S(2)}) %collective-permute-start.14) | collective-permute-done | bytes 65568 | tf_op jit(solution)/shard_map/ppermute | solution.py:533
  71.8 1.2 %collective-permute-done.15.got_ref = f32[1,64,128]{2,1,0:T(8,128)S(1)} collective-permute-done((f32[1,64,128]{2,1,0:T(8,128)S(1)}, f32[1,64,128]{2,1,0:T(8,128)S(1)}, u32[]{:S(2)}, u32[]{:S(2)}) %collective-permute-start.15) | collective-permute-done | bytes 32800 | tf_op jit(solution)/shard_map/ppermute | solution.py:430
  73.0 2.7 %collective-permute-start.16 = (f32[1,64,128]{2,1,0:T(8,128)S(1)}, f32[1,64,128]{2,1,0:T(8,128)S(1)}, u32[]{:S(2)}, u32[]{:S(2)}) collective-permute-start(f32[1,64,128]{2,1,0:T(8,128)S(1)} %get-tuple-element.121), channel_id=1, source_target_pairs={{0,16},{8,24},{16,0},{24,8},{1,17},{9,25},{17,1},{25,9},{2,18},{10... | collective-permute-start | bytes 98312 | tf_op jit(solution)/shard_map/ppermute | solution.py:542
  75.7 2.6 %collective-permute-done.16.refs_1_ = f32[1,64,128]{2,1,0:T(8,128)S(1)} collective-permute-done((f32[1,64,128]{2,1,0:T(8,128)S(1)}, f32[1,64,128]{2,1,0:T(8,128)S(1)}, u32[]{:S(2)}, u32[]{:S(2)}) %collective-permute-start.16) | collective-permute-done | bytes 32800 | tf_op jit(solution)/shard_map/ppermute | solution.py:542
  (28 shorter events, 6.9 us)
Async XLA Ops:
  0.6 2.8 %copy-start = (s32[1,8]{1,0:T(1,128)S(1)}, s32[1,8]{1,0:T(1,128)}, u32[]{:S(2)}) copy-start(s32[1,8]{1,0:T(1,128)} %len_ref.1) | copy-start | bytes 100
  2.3 2.1 %collective-permute-start.2 = (f32[128,1024]{1,0:T(8,128)S(1)}, f32[128,1024]{1,0:T(8,128)S(1)}, u32[]{:S(2)}, u32[]{:S(2)}) collective-permute-start(f32[128,1024]{1,0:T(8,128)S(1)} %get-tuple-element.72), channel_id=1, source_target_pairs={{0,1},{1,0},{2,3},{3,2},{4,5},{5,4},{6,7},{7,6},{8,9},{9,8},{10,11... | collective-permute-start | bytes 1572872 | tf_op jit(solution)/shard_map/ppermute | solution.py:430
  2.9 2.3 %collective-permute-start.3 = (f32[128,1024]{1,0:T(8,128)S(1)}, f32[128,1024]{1,0:T(8,128)S(1)}, u32[]{:S(2)}, u32[]{:S(2)}) collective-permute-start(f32[128,1024]{1,0:T(8,128)S(1)} %get-tuple-element.73), channel_id=1, source_target_pairs={{0,1},{1,0},{2,3},{3,2},{4,5},{5,4},{6,7},{7,6},{8,9},{9,8},{10,11... | collective-permute-start | bytes 1572872 | tf_op jit(solution)/shard_map/ppermute | solution.py:430
  3.0 10.0 %collective-permute-start = (f32[128,1024]{1,0:T(8,128)S(1)}, f32[128,1024]{1,0:T(8,128)S(1)}, u32[]{:S(2)}, u32[]{:S(2)}) collective-permute-start(f32[128,1024]{1,0:T(8,128)S(1)} %get-tuple-element.67), channel_id=1, source_target_pairs={{0,1},{1,0},{2,3},{3,2},{4,5},{5,4},{6,7},{7,6},{8,9},{9,8},{10,11... | collective-permute-start | bytes 1572872 | tf_op jit(solution)/shard_map/ppermute | solution.py:430
  3.4 9.6 %collective-permute-start.1 = (f32[128,1024]{1,0:T(8,128)S(1)}, f32[128,1024]{1,0:T(8,128)S(1)}, u32[]{:S(2)}, u32[]{:S(2)}) collective-permute-start(f32[128,1024]{1,0:T(8,128)S(1)} %get-tuple-element.68), channel_id=1, source_target_pairs={{0,1},{1,0},{2,3},{3,2},{4,5},{5,4},{6,7},{7,6},{8,9},{9,8},{10,11... | collective-permute-start | bytes 1572872 | tf_op jit(solution)/shard_map/ppermute | solution.py:430
  8.2 7.9 %collective-permute-start.4 = (f32[264,128]{1,0:T(8,128)S(1)}, f32[264,128]{1,0:T(8,128)S(1)}, u32[]{:S(2)}, u32[]{:S(2)}) collective-permute-start(f32[264,128]{1,0:T(8,128)S(1)} %get-tuple-element.79), channel_id=1, source_target_pairs={{0,2},{1,3},{2,4},{3,5},{4,6},{5,7},{8,10},{9,11},{10,12},{11,13},... | collective-permute-start | bytes 405512 | tf_op jit(solution)/shard_map/ppermute | solution.py:463
  17.6 29.2 %collective-permute-start.5 = (f32[8,128,128]{2,1,0:T(8,128)S(1)}, f32[8,128,128]{2,1,0:T(8,128)S(1)}, u32[]{:S(2)}, u32[]{:S(2)}) collective-permute-start(f32[8,128,128]{2,1,0:T(8,128)S(1)} %get-tuple-element.80), channel_id=1, source_target_pairs={{2,0},{3,1},{4,2},{5,3},{6,4},{7,5},{10,8},{11,9},{12,10},{13,11},... | collective-permute-start | bytes 1572872 | tf_op jit(solution)/shard_map/ppermute | solution.py:463
  18.9 12.8 %collective-permute-start.6 = (f32[6,128,128]{2,1,0:T(8,128)S(1)}, f32[6,128,128]{2,1,0:T(8,128)S(1)}, u32[]{:S(2)}, u32[]{:S(2)}) collective-permute-start(f32[6,128,128]{2,1,0:T(8,128)S(1)} %get-tuple-element.81), channel_id=1, source_target_pairs={{0,2},{1,3},{2,4},{3,5},{4,6},{5,7},{8,10},{9,11},{10,12},{11,13},... | collective-permute-start | bytes 1179656 | tf_op jit(solution)/shard_map/ppermute | solution.py:463
  33.7 13.1 %collective-permute-start.7 = (f32[8,1,128]{2,1,0:T(1,128)S(1)}, f32[8,1,128]{2,1,0:T(1,128)S(1)}, u32[]{:S(2)}, u32[]{:S(2)}) collective-permute-start(f32[8,1,128]{2,1,0:T(1,128)S(1)} %get-tuple-element.88), channel_id=1, source_target_pairs={{2,0},{3,1},{4,2},{5,3},{6,4},{7,5},{10,8},{11,9},{12,10},{13,11},... | collective-permute-start | bytes 12296 | tf_op jit(solution)/shard_map/ppermute | solution.py:463
  49.6 15.3 %collective-permute-start.11 = (f32[128,1024]{1,0:T(8,128)S(1)}, f32[128,1024]{1,0:T(8,128)S(1)}, u32[]{:S(2)}, u32[]{:S(2)}) collective-permute-start(f32[128,1024]{1,0:T(8,128)S(1)} %get-tuple-element.108), channel_id=1, source_target_pairs={{0,1},{1,0},{2,3},{3,2},{4,5},{5,4},{6,7},{7,6},{8,9},{9,8},{10,11... | collective-permute-start | bytes 1572872 | tf_op jit(solution)/shard_map/ppermute | solution.py:430
  49.6 16.1 %collective-permute-start.12 = (f32[128,1024]{1,0:T(8,128)S(1)}, f32[128,1024]{1,0:T(8,128)S(1)}, u32[]{:S(2)}, u32[]{:S(2)}) collective-permute-start(f32[128,1024]{1,0:T(8,128)S(1)} %get-tuple-element.110), channel_id=1, source_target_pairs={{0,1},{1,0},{2,3},{3,2},{4,5},{5,4},{6,7},{7,6},{8,9},{9,8},{10,11... | collective-permute-start | bytes 1572872 | tf_op jit(solution)/shard_map/ppermute | solution.py:430
  50.1 16.5 %collective-permute-start.13 = (f32[128,1024]{1,0:T(8,128)S(1)}, f32[128,1024]{1,0:T(8,128)S(1)}, u32[]{:S(2)}, u32[]{:S(2)}) collective-permute-start(f32[128,1024]{1,0:T(8,128)S(1)} %get-tuple-element.112), channel_id=1, source_target_pairs={{0,1},{1,0},{2,3},{3,2},{4,5},{5,4},{6,7},{7,6},{8,9},{9,8},{10,11... | collective-permute-start | bytes 1572872 | tf_op jit(solution)/shard_map/ppermute | solution.py:430
  50.2 7.5 %collective-permute-start.8 = (f32[2,128,128]{2,1,0:T(8,128)S(1)}, f32[2,128,128]{2,1,0:T(8,128)S(1)}, u32[]{:S(2)}, u32[]{:S(2)}) collective-permute-start(f32[2,128,128]{2,1,0:T(8,128)S(1)} %get-tuple-element.100), channel_id=1, source_target_pairs={{0,2},{1,3},{2,0},{3,1},{4,6},{5,7},{6,4},{7,5},{8,10},{9,11},{10,... | collective-permute-start | bytes 393224 | tf_op jit(solution)/shard_map/ppermute | solution.py:515
  53.6 8.0 %collective-permute-start.9 = (f32[2,128,128]{2,1,0:T(8,128)S(1)}, f32[2,128,128]{2,1,0:T(8,128)S(1)}, u32[]{:S(2)}, u32[]{:S(2)}) collective-permute-start(f32[2,128,128]{2,1,0:T(8,128)S(1)} %get-tuple-element.101), channel_id=1, source_target_pairs={{0,4},{1,5},{2,6},{3,7},{4,0},{5,1},{6,2},{7,3},{8,12},{9,13},{10,... | collective-permute-start | bytes 393224 | tf_op jit(solution)/shard_map/ppermute | solution.py:515
  57.7 7.2 %collective-permute-start.10 = (f32[2,128,128]{2,1,0:T(8,128)S(1)}, f32[2,128,128]{2,1,0:T(8,128)S(1)}, u32[]{:S(2)}, u32[]{:S(2)}) collective-permute-start(f32[2,128,128]{2,1,0:T(8,128)S(1)} %get-tuple-element.102), channel_id=1, source_target_pairs={{0,6},{1,7},{2,4},{3,5},{4,2},{5,3},{6,0},{7,1},{8,14},{9,15},{10,... | collective-permute-start | bytes 393224 | tf_op jit(solution)/shard_map/ppermute | solution.py:515
  67.4 4.3 %collective-permute-start.14 = (f32[1,128,128]{2,1,0:T(8,128)S(1)}, f32[1,128,128]{2,1,0:T(8,128)S(1)}, u32[]{:S(2)}, u32[]{:S(2)}) collective-permute-start(f32[1,128,128]{2,1,0:T(8,128)S(1)} %get-tuple-element.117), channel_id=1, source_target_pairs={{0,8},{8,0},{16,24},{24,16},{1,9},{9,1},{17,25},{25,17},{2,10},{10... | collective-permute-start | bytes 196616 | tf_op jit(solution)/shard_map/ppermute | solution.py:533
  71.7 1.3 %collective-permute-start.15 = (f32[1,64,128]{2,1,0:T(8,128)S(1)}, f32[1,64,128]{2,1,0:T(8,128)S(1)}, u32[]{:S(2)}, u32[]{:S(2)}) collective-permute-start(f32[1,64,128]{2,1,0:T(8,128)S(1)} %get-tuple-element.119), channel_id=1, source_target_pairs={{0,1},{1,0},{2,3},{3,2},{4,5},{5,4},{6,7},{7,6},{8,9},{9,8},{10,11... | collective-permute-start | bytes 98312 | tf_op jit(solution)/shard_map/ppermute | solution.py:430
  73.0 5.2 %collective-permute-start.16 = (f32[1,64,128]{2,1,0:T(8,128)S(1)}, f32[1,64,128]{2,1,0:T(8,128)S(1)}, u32[]{:S(2)}, u32[]{:S(2)}) collective-permute-start(f32[1,64,128]{2,1,0:T(8,128)S(1)} %get-tuple-element.121), channel_id=1, source_target_pairs={{0,16},{8,24},{16,0},{24,8},{1,17},{9,25},{17,1},{25,9},{2,18},{10... | collective-permute-start | bytes 98312 | tf_op jit(solution)/shard_map/ppermute | solution.py:542
